TPU v7x, 32 devices: a whole 2x2x4 slice. The times are simulated.
32 devices in a mesh: seq: 8 (over z, core), head: 4 (over y, x).
Axes of the slice: x: 2, y: 2, z: 4, core: 2. Of those that a mesh axis runs over, the one named last changes fastest.
Arguments:
- attn_query: bfloat16 [16384, 2560], P('seq', 'head'), may hold values from -45 to 45
- attn_key: bfloat16 [16384, 2560], P('seq', 'head'), may hold values from -15 to 15
- attn_value: bfloat16 [16384, 2560], P('seq', 'head'), may hold values from -6 to 6
- fast_query: bfloat16 [16384, 2560], P('seq', 'head'), may hold values from -6 to 6
- fast_key: bfloat16 [16384, 2560], P('seq', 'head'), may hold values from -6 to 6
- fast_value: bfloat16 [16384, 2560], P('seq', 'head'), may hold values from -6 to 6
- rates: float32 [16384, 4], P('seq', 'head'), may hold values from 0.00022097086 to 0.0022097088
- fast_weights: float32 [4, 640, 3, 640], P('head'), may hold values from -0.25 to 0.25
- gain: float32 [4, 640], P('head'), may hold values from 0.5 to 1.5
Outputs:
- mixed: bfloat16 [16384, 2560], P('seq', 'head')
- final_weights: float32 [4, 640, 3, 640], P('head', 'seq')
All inputs are finite; a program needn't handle non-finite values.
Results may differ from a plain program's by a relative error of at most 0.013.
Values may be sent and summed in bfloat16 or wider, within the bound.
A program may use at most 192 MiB of HBM per device.

v0:
```python
import functools
import math

import jax
import jax.numpy as jnp
from jax import lax
from jax.experimental import pallas as pl
from jax.experimental.pallas import tpu as pltpu
from jax.sharding import PartitionSpec as P

AH = 128
WINDOW = 512
EPSILON = 1e-06
NEG = -1e30
NT = (((1,), (1,)), ((), ()))
NN = (((1,), (0,)), ((), ()))
LIMIT = 60 * 1024 * 1024


def mm(a, b, dims):
    return lax.dot_general(a, b, dims, preferred_element_type=jnp.float32)


def sigmoid(v):
    return 0.5 * jnp.tanh(0.5 * v) + 0.5


def attend(q, keys, values, biases):
    rows = q.shape[0]
    factor = math.log2(math.e) / math.sqrt(AH)
    old, mid, new = (mm(q, k, NT) for k in keys)
    if biases[0] is not None:
        old = old + biases[0]
    if biases[1] is not None:
        mid = mid + biases[1]
    row = lax.broadcasted_iota(jnp.int32, (rows, rows), 0)
    col = lax.broadcasted_iota(jnp.int32, (rows, rows), 1)
    causal = col <= row
    edge = jnp.where(causal, new, old)
    top = jnp.maximum(jnp.max(edge, -1, keepdims=True), jnp.max(mid, -1, keepdims=True))
    edge = jnp.exp2((edge - top) * factor)
    mid = jnp.exp2((mid - top) * factor)
    total = jnp.sum(edge, -1, keepdims=True) + jnp.sum(mid, -1, keepdims=True)
    p_new = jnp.where(causal, edge, 0.0).astype(jnp.bfloat16)
    p_old = jnp.where(causal, 0.0, edge).astype(jnp.bfloat16)
    out = mm(p_new, values[2], NN) + mm(p_old, values[0], NN)
    out = out + mm(mid.astype(jnp.bfloat16), values[1], NN)
    return out * (1.0 / total)


def attention_kernel(q_ref, k_ref, v_ref, hk_ref, hv_ref, o_ref):
    tile = WINDOW // 2
    bias = jnp.where(lax.axis_index("seq") == 0, jnp.float32(NEG), jnp.float32(0.0))

    def block(ref, halo, at):
        if at < 0:
            return halo[(at + 2) * tile : (at + 3) * tile, :]
        return ref[at * tile : (at + 1) * tile, :]

    for t in range(q_ref.shape[0] // tile):
        keys = [block(k_ref, hk_ref, t - 2 + i) for i in range(3)]
        values = [block(v_ref, hv_ref, t - 2 + i) for i in range(3)]
        biases = [bias if t - 2 + i < 0 else None for i in range(2)]
        o_ref[t * tile : (t + 1) * tile, :] = attend(
            q_ref[t * tile : (t + 1) * tile, :], keys, values, biases
        )


def attention(q, k, v, hk, hv):
    rows, columns = q.shape
    part = pl.BlockSpec((rows, AH), lambda h: (0, h))
    halo = pl.BlockSpec((WINDOW, AH), lambda h: (0, h))
    return pl.pallas_call(
        attention_kernel,
        grid=(columns // AH,),
        out_shape=jax.ShapeDtypeStruct((rows, columns), jnp.float32),
        in_specs=[part, part, part, halo, halo],
        out_specs=part,
        compiler_params=pltpu.CompilerParams(vmem_limit_bytes=LIMIT),
        cost_estimate=pl.CostEstimate(
            flops=4 * rows * columns * WINDOW * 4, bytes_accessed=10 * rows * columns, transcendentals=0
        ),
    )(q, k, v, hk, hv)


def grad_parts(w_ref, x, val, rate):
    signal = (rate * val.astype(jnp.float32)).astype(jnp.bfloat16)
    gate = mm(w_ref[0], x, NT)
    up = mm(w_ref[1], x, NT)
    back = mm(w_ref[2], signal, NT)
    s = sigmoid(gate)
    active = gate * s
    hidden = (active * up).astype(jnp.bfloat16)
    up_grad = (back * active).astype(jnp.bfloat16)
    gate_grad = (back * up * (s * (1.0 + gate * (1.0 - s)))).astype(jnp.bfloat16)
    return mm(gate_grad, x, NN), mm(up_grad, x, NN), mm(hidden, signal, NN)


def gradient_kernel(block, half, w_ref, x_ref, val_ref, rate_ref, o_ref, acc):
    active = lax.axis_index("seq") // half == block
    step = pl.program_id(0)
    last = pl.num_programs(0) - 1

    @pl.when(active)
    def _():
        parts = grad_parts(w_ref, x_ref[...], val_ref[...], rate_ref[...])
        for i in range(3):
            @pl.when(step == 0)
            def _():
                acc[i] = parts[i]

            @pl.when(step > 0)
            def _():
                acc[i] += parts[i]

            @pl.when(step == last)
            def _():
                o_ref[i] = acc[i].astype(o_ref.dtype)

    @pl.when(jnp.logical_not(active) & (step == last))
    def _():
        o_ref[...] = jnp.zeros_like(o_ref)


def gradient(block, half, w, x, val, rate):
    rows, d = x.shape
    f = w.shape[1]
    m = min(rows, 512)
    return pl.pallas_call(
        functools.partial(gradient_kernel, block, half),
        grid=(rows // m,),
        out_shape=jax.ShapeDtypeStruct((3, f, d), jnp.bfloat16),
        in_specs=[
            pl.BlockSpec((3, f, d), lambda i: (0, 0, 0)),
            pl.BlockSpec((m, d), lambda i: (i, 0)),
            pl.BlockSpec((m, d), lambda i: (i, 0)),
            pl.BlockSpec((m, 1), lambda i: (i, 0)),
        ],
        out_specs=pl.BlockSpec((3, f, d), lambda i: (0, 0, 0)),
        scratch_shapes=[pltpu.VMEM((3, f, d), jnp.float32)],
        compiler_params=pltpu.CompilerParams(vmem_limit_bytes=LIMIT),
    )(w, x, val, rate)


def apply_tile(w_ref, x, gain):
    gate = mm(x, w_ref[0], NT)
    up = mm(x, w_ref[1], NT)
    hidden = (gate * sigmoid(gate) * up).astype(jnp.bfloat16)
    out = mm(hidden, w_ref[2], NN)
    inverse = lax.rsqrt(jnp.mean(out * out, axis=-1, keepdims=True) + EPSILON)
    return out * inverse * gain


def apply_kernel(w_ref, x_ref, gain_ref, att_ref, o_ref):
    o_ref[...] = (att_ref[...] + apply_tile(w_ref, x_ref[...], gain_ref[...])).astype(o_ref.dtype)


def apply(w, x, gain, attended):
    rows, d = x.shape
    f = w.shape[1]
    m = min(rows, 512)
    tile = pl.BlockSpec((m, d), lambda i: (i, 0))
    return pl.pallas_call(
        apply_kernel,
        grid=(rows // m,),
        out_shape=jax.ShapeDtypeStruct((rows, d), jnp.bfloat16),
        in_specs=[
            pl.BlockSpec((3, f, d), lambda i: (0, 0, 0)),
            tile,
            pl.BlockSpec((1, d), lambda i: (0, 0)),
            tile,
        ],
        out_specs=tile,
        compiler_params=pltpu.CompilerParams(vmem_limit_bytes=LIMIT),
        cost_estimate=pl.CostEstimate(flops=12 * rows * d * f, bytes_accessed=10 * rows * d, transcendentals=0),
    )(w, x, gain, attended)


def renormalize(previous, grad):
    moved = previous + grad
    return moved * (
        jnp.sqrt(jnp.mean(previous * previous, axis=-1, keepdims=True) + EPSILON)
        / jnp.sqrt(jnp.mean(moved * moved, axis=-1, keepdims=True) + EPSILON)
    )


def shards(
    attn_query, attn_key, attn_value, fast_query, fast_key, fast_value, rates, fast_weights, gain
):
    count = lax.axis_size("seq")
    seq = lax.axis_index("seq")
    half = count // 2
    pairs = [(i, i + 1) for i in range(count - 1)]
    halo_k, halo_v = lax.ppermute((attn_key[-WINDOW:], attn_value[-WINDOW:]), "seq", pairs)
    initial = jnp.swapaxes(fast_weights[0], 0, 1)
    first_cast = initial.astype(jnp.bfloat16)
    share = initial.shape[1] // count

    first = gradient(0, half, first_cast, fast_key, fast_value, rates)
    first_part = lax.psum_scatter(first, "seq", scatter_dimension=1, tiled=True)
    attended = attention(attn_query, attn_key, attn_value, halo_k, halo_v)
    middle_rows = renormalize(
        lax.dynamic_slice_in_dim(initial, seq * share, share, 1), first_part.astype(jnp.float32)
    )
    middle_cast = lax.all_gather(middle_rows.astype(jnp.bfloat16), "seq", axis=1, tiled=True)
    second = gradient(1, half, middle_cast, fast_key, fast_value, rates)
    second_part = lax.psum_scatter(second, "seq", scatter_dimension=1, tiled=True)
    mixed = apply(jnp.where(seq < half, first_cast, middle_cast), fast_query, gain, attended)
    final_rows = renormalize(middle_rows, second_part.astype(jnp.float32))
    return (mixed, jnp.swapaxes(final_rows, 0, 1)[None])


def solution(mesh):
    tokens = P("seq", "head")
    in_specs = (tokens,) * 7 + (P("head", None, None, None), P("head", None))
    out_specs = (tokens, P("head", "seq", None, None))
    return jax.shard_map(shards, mesh=mesh, in_specs=in_specs, out_specs=out_specs, check_vma=False)
```

profile of v0, /device:TPU:16, one launch (start us, length us, event | category | flops | bytes accessed | tf_op | source)
XLA Modules:
  0.0 210.8 jit_solution(17673522428254089285)
XLA Ops:
  7.2 0.0 reduce-scatter.3.cloned.1.call-start
  7.2 2.0 copy.11.rate_ref
  9.3 4.1 %convert_bitcast_fusion.w_ref = bf16[3,640,640]{2,1,0:T(8,128)(2,1)} fusion(f32[1,640,3,640]{3,1,2,0:T(8,128)} %param.16), kind=kLoop, calls=%fused_computation | loop fusion | flops 1228800 | bytes 7372800 | tf_op jit(solution)/shard_map/convert_element_type | solution.py:196
  13.3 6.0 %shard_map.104 = bf16[3,640,640]{2,1,0:T(8,128)(2,1)} custom-call(bf16[3,640,640]{2,1,0:T(8,128)(2,1)} %convert_bitcast_fusion.w_ref, bf16[2048,640]{1,0:T(8,128)(2,1)} %x_ref.5, bf16[2048,640]{1,0:T(8,128)(2,1)} %val_ref.3, f32[2048,1]{1,0:T(8,128)} %copy.11.rate_ref), custom_call_target="tpu_custom_call" | custom-call | tf_op jit(solution)/shard_map/pallas_call | solution.py:129
  19.4 0.0 reduce-scatter.3.cloned.1.call-update
  19.4 0.0 all-gather.2.cloned.1.call-start
  19.5 44.1 %reduce-scatter.3.cloned.1.call-done = bf16[3,80,640]{2,1,0:T(8,128)(2,1)} async-done(((bf16[3,640,640]{2,1,0:T(8,128)(2,1)}), bf16[3,80,640]{2,1,0:T(8,128)(2,1)}) %reduce-scatter.3.cloned.1.call-update) | async-done | bytes 307216 | tf_op jit(solution)/shard_map/reduce_scatter | solution.py:200
  63.5 1.4 multiply_reduce_fusion.2
  64.9 0.8 multiply_convert_fusion
  65.8 0.0 all-gather.2.cloned.1.call-update
  65.8 0.0 reduce-scatter.5.cloned.1.call-start
  65.8 36.9 %all-gather.2.cloned.1.call-done.w_ref = bf16[3,640,640]{2,1,0:T(8,128)(2,1)} async-done(((bf16[3,80,640]{2,1,0:T(8,128)(2,1)}), bf16[3,640,640]{2,1,0:T(8,128)(2,1)}) %all-gather.2.cloned.1.call-update) | async-done | bytes 2457616 | tf_op jit(solution)/shard_map/all_gather | solution.py:205
  102.7 19.9 %shard_map.107 = bf16[3,640,640]{2,1,0:T(8,128)(2,1)} custom-call(bf16[3,640,640]{2,1,0:T(8,128)(2,1)} %all-gather.2.cloned.1.call-done.w_ref, bf16[2048,640]{1,0:T(8,128)(2,1)} %x_ref.5, bf16[2048,640]{1,0:T(8,128)(2,1)} %val_ref.3, f32[2048,1]{1,0:T(8,128)} %copy.11.rate_ref), custom_call_target="tpu_custom_call" | custom-call | tf_op jit(solution)/shard_map/pallas_call | solution.py:129
  122.7 1.1 slice.7
  123.8 2.1 %collective-permute-start.1 = (bf16[512,640]{1,0:T(8,128)(2,1)S(1)}, bf16[512,640]{1,0:T(8,128)(2,1)}, u32[]{:S(2)}, u32[]{:S(2)}) collective-permute-start(bf16[512,640]{1,0:T(8,128)(2,1)S(1)} %slice.7), channel_id=1, source_target_pairs={{0,4},{4,8},{8,12},{12,16},{16,20},{20,24},{24,28},{1,5},{5,9},{9,... | collective-permute-start | bytes 1966088 | tf_op jit(solution)/shard_map/ppermute | solution.py:194
  126.0 2.0 slice.6
  127.9 2.6 %collective-permute-start = (bf16[512,640]{1,0:T(8,128)(2,1)}, bf16[512,640]{1,0:T(8,128)(2,1)}, u32[]{:S(2)}, u32[]{:S(2)}) collective-permute-start(bf16[512,640]{1,0:T(8,128)(2,1)} %slice.6), channel_id=1, source_target_pairs={{0,4},{4,8},{8,12},{12,16},{16,20},{20,24},{24,28},{1,5},{5,9},{9,... | collective-permute-start | bytes 1966088 | tf_op jit(solution)/shard_map/ppermute | solution.py:194
  130.5 19.0 %collective-permute-done.1.hv_ref = bf16[512,640]{1,0:T(8,128)(2,1)} collective-permute-done((bf16[512,640]{1,0:T(8,128)(2,1)S(1)}, bf16[512,640]{1,0:T(8,128)(2,1)}, u32[]{:S(2)}, u32[]{:S(2)}) %collective-permute-start.1) | collective-permute-done | bytes 655392 | tf_op jit(solution)/shard_map/ppermute | solution.py:194
  149.6 16.6 %collective-permute-done.hk_ref = bf16[512,640]{1,0:T(8,128)(2,1)} collective-permute-done((bf16[512,640]{1,0:T(8,128)(2,1)}, bf16[512,640]{1,0:T(8,128)(2,1)}, u32[]{:S(2)}, u32[]{:S(2)}) %collective-permute-start) | collective-permute-done | bytes 655392 | tf_op jit(solution)/shard_map/ppermute | solution.py:194
  166.1 18.8 %shard_map.105.att_ref = f32[2048,640]{1,0:T(8,128)} custom-call(bf16[2048,640]{1,0:T(8,128)(2,1)} %q_ref.1, bf16[2048,640]{1,0:T(8,128)(2,1)} %k_ref.1, bf16[2048,640]{1,0:T(8,128)(2,1)} %v_ref.1, bf16[512,640]{1,0:T(8,128)(2,1)} %collective-permute-done.hk_ref, bf16[512,640]{1,0:T(8,128)(2,1)} %collective-permute-done.1.hv_ref), custom_call_target="tpu_custom_call" | custom-call | flops 10737418240 | bytes 13107200 | tf_op jit(solution)/shard_map/pallas_call | solution.py:73
  184.9 4.4 %broadcast_select_fusion.w_ref = bf16[3,640,640]{2,1,0:T(8,128)(2,1)} fusion(bf16[3,640,640]{2,1,0:T(8,128)(2,1)S(1)} %copy-done, pred[]{:T(512)S(6)} %lt.6, f32[1,640,3,640]{3,1,2,0:T(8,128)} %param.16), kind=kLoop, calls=%fused_computation.1 | loop fusion | flops 2457600 | bytes 9830401 | tf_op jit(solution)/shard_map/jit(_where)/select_n | solution.py:208
  189.3 11.8 %shard_map.106 = bf16[2048,640]{1,0:T(8,128)(2,1)} custom-call(bf16[3,640,640]{2,1,0:T(8,128)(2,1)} %broadcast_select_fusion.w_ref, bf16[2048,640]{1,0:T(8,128)(2,1)} %x_ref.4, f32[1,640]{1,0:T(1,128)} %gain_ref.1, f32[2048,640]{1,0:T(8,128)} %shard_map.105.att_ref), custom_call_target="tpu_custom_call" | custom-call | flops 10066329600 | bytes 13107200 | tf_op jit(solution)/shard_map/pallas_call | solution.py:163
  201.1 1.3 multiply_reduce_fusion.1
  202.3 1.9 multiply_bitcast_fusion
  (6 shorter events, 0.0 us)
Async XLA Ops:
  7.2 56.4 %reduce-scatter.3.cloned.1.call-start = ((), (), s32[]{:S(2)}) async-start(), calls=%async_computation.2 | async-start | bytes 2764800 | tf_op jit(solution)/shard_map/reduce_scatter | solution.py:200
  19.4 83.3 %all-gather.2.cloned.1.call-start = ((), (), s32[]{:S(2)}) async-start(), calls=%async_computation.3 | async-start | bytes 2764800 | tf_op jit(solution)/shard_map/all_gather | solution.py:205
  65.8 135.3 %reduce-scatter.5.cloned.1.call-start = ((), (), s32[]{:S(2)}) async-start(), calls=%async_computation.4 | async-start | bytes 2764800 | tf_op jit(solution)/shard_map/reduce_scatter | solution.py:207
  123.8 25.8 %collective-permute-start.1 = (bf16[512,640]{1,0:T(8,128)(2,1)S(1)}, bf16[512,640]{1,0:T(8,128)(2,1)}, u32[]{:S(2)}, u32[]{:S(2)}) collective-permute-start(bf16[512,640]{1,0:T(8,128)(2,1)S(1)} %slice.7), channel_id=1, source_target_pairs={{0,4},{4,8},{8,12},{12,16},{16,20},{20,24},{24,28},{1,5},{5,9},{9,... | collective-permute-start | bytes 1966088 | tf_op jit(solution)/shard_map/ppermute | solution.py:194
  127.9 38.2 %collective-permute-start = (bf16[512,640]{1,0:T(8,128)(2,1)}, bf16[512,640]{1,0:T(8,128)(2,1)}, u32[]{:S(2)}, u32[]{:S(2)}) collective-permute-start(bf16[512,640]{1,0:T(8,128)(2,1)} %slice.6), channel_id=1, source_target_pairs={{0,4},{4,8},{8,12},{12,16},{16,20},{20,24},{24,28},{1,5},{5,9},{9,... | collective-permute-start | bytes 1966088 | tf_op jit(solution)/shard_map/ppermute | solution.py:194
  130.5 54.4 %copy-start = (bf16[3,640,640]{2,1,0:T(8,128)(2,1)S(1)}, bf16[3,640,640]{2,1,0:T(8,128)(2,1)}, u32[]{:S(2)}) copy-start(bf16[3,640,640]{2,1,0:T(8,128)(2,1)} %all-gather.2.cloned.1.call-done.w_ref) | copy-start | bytes 7372804
Sparse Core Ops, SparseCore 0:
  19.5 43.9 reduce-scatter.2
  65.9 36.7 all-gather.1
  122.8 43.0 reduce-scatter.4
where the time goes:
time: 211 us
  waiting for transfers between devices  117 us (55%)
  Pallas kernels  56.5 us (27%)
  other arithmetic  13.9 us (7%)
  between operations  13.8 us (7%)
  local copies, waits for them, and re-layouts  5.18 us (2%)
  starting transfers between devices  4.84 us (2%)
    reduce_scatter x1, waiting for transfers between devices, shards(): first_part = lax.psum_scatter(first, 'seq', scatter_dimension=1, tiled=True)  44.1 us
    all_gather x1, waiting for transfers between devices, shards(): lax.all_gather(middle_rows.astype(jnp.bfloat16), 'seq', axis=1, tiled=True)  36.9 us
    ppermute x2, waiting for transfers between devices, shards(): lax.ppermute((attn_key[-WINDOW:], attn_value[-WINDOW:]), 'seq', pairs)  35.6 us
    pallas_call x2, Pallas kernels, gradient(): pl.pallas_call(functools.partial(gradient_kernel, block, half), grid=(row...  26 us
    pallas_call x1, Pallas kernels, attention(): pl.pallas_call(attention_kernel, grid=(columns // AH,), out_shape=jax.Sha...  18.8 us
    pallas_call x1, Pallas kernels, apply(): pl.pallas_call(apply_kernel, grid=(rows // m,), out_shape=jax.ShapeDtypeS...  11.8 us
    ppermute x2, starting transfers between devices, shards(): lax.ppermute((attn_key[-WINDOW:], attn_value[-WINDOW:]), 'seq', pairs)  4.72 us
    select_n x1, other arithmetic, shards(): jnp.where(seq < half, first_cast, middle_cast)  4.38 us
  transfers between devices with their start and end apart: 5, of which 4 were waited for; matrix products, arithmetic and copies ran while one was open for 4% of the time, Pallas kernels for 14%

commit v1 on v0

v1 whole, which is shorter than its diff:
```python
import functools
import math
from types import SimpleNamespace

import jax
import jax.numpy as jnp
from jax import lax
from jax.experimental import pallas as pl
from jax.experimental.pallas import tpu as pltpu
from jax.sharding import PartitionSpec as P

AH = 128
WINDOW = 512
EPSILON = 1e-06
NEG = -1e30
NT = (((1,), (1,)), ((), ()))
NN = (((1,), (0,)), ((), ()))
LIMIT = 62 * 1024 * 1024
UNIT = 32
PACK = 2
TILE = 1024
BF = jnp.bfloat16
F32 = jnp.float32


def mm(a, b, dims):
    return lax.dot_general(a, b, dims, preferred_element_type=jnp.float32)


def sigmoid(v):
    return 0.5 * jnp.tanh(0.5 * v) + 0.5


def attend(q, keys, values, biases):
    rows = q.shape[0]
    factor = math.log2(math.e) / math.sqrt(AH)
    old, mid, new = (mm(q, k, NT) for k in keys)
    if biases[0] is not None:
        old = old + biases[0]
    if biases[1] is not None:
        mid = mid + biases[1]
    row = lax.broadcasted_iota(jnp.int32, (rows, rows), 0)
    col = lax.broadcasted_iota(jnp.int32, (rows, rows), 1)
    causal = col <= row
    edge = jnp.where(causal, new, old)
    top = jnp.maximum(jnp.max(edge, -1, keepdims=True), jnp.max(mid, -1, keepdims=True))
    edge = jnp.exp2((edge - top) * factor)
    mid = jnp.exp2((mid - top) * factor)
    total = jnp.sum(edge, -1, keepdims=True) + jnp.sum(mid, -1, keepdims=True)
    p_new = jnp.where(causal, edge, 0.0).astype(BF)
    p_old = jnp.where(causal, 0.0, edge).astype(BF)
    out = mm(p_new, values[2], NN) + mm(p_old, values[0], NN)
    out = out + mm(mid.astype(BF), values[1], NN)
    return out * (1.0 / total)


def renormalize(previous, grad):
    moved = previous + grad
    return moved * (
        jnp.sqrt(jnp.mean(previous * previous, axis=-1, keepdims=True) + EPSILON)
        / jnp.sqrt(jnp.mean(moved * moved, axis=-1, keepdims=True) + EPSILON)
    )


def sizes(count, rows, d, f, columns):
    half = count // 2
    chips = half // 2
    rpo = UNIT // chips
    share = f // count
    per_block = share // rpo
    groups = 2 * per_block
    z = SimpleNamespace(
        count=count, half=half, chips=chips, rpo=rpo, share=share, nb=per_block, ng=groups,
        ns=groups // PACK, rows=rows, d=d, heads=columns // AH,
    )
    assert z.rpo * z.chips == UNIT and z.nb * z.rpo == z.share and z.ns * PACK == z.ng
    assert z.heads == z.ns and z.ns >= 3 + (z.nb - 1) // PACK
    return z


def scratch(z):
    unit = (3, UNIT, z.d)
    piece = (3, z.rpo, z.d)
    tokens = pltpu.VMEM((z.rows, z.d), BF)
    halo = pltpu.VMEM((WINDOW, z.d), BF)
    dma = pltpu.SemaphoreType.DMA
    return dict(
        qs=tokens, ks=tokens, vs=tokens, fqs=tokens, xs=tokens, ys=tokens, outs=tokens,
        att=pltpu.VMEM((z.rows, z.d), F32),
        app=pltpu.VMEM((z.rows, z.d), F32),
        hk=halo, hv=halo,
        wf=pltpu.VMEM((z.ng, 2, 3, z.chips, z.rpo, z.d), F32),
        wb=pltpu.VMEM((z.ng, 2) + unit, BF),
        acc=pltpu.VMEM((PACK, 2) + unit, F32),
        gsum=pltpu.VMEM((z.ng,) + unit, F32),
        pair_s=pltpu.VMEM((z.ng,) + unit, BF),
        pair_r=pltpu.VMEM((z.ng,) + unit, BF),
        chain_s=pltpu.VMEM((z.ng,) + unit, BF),
        chain_r=pltpu.VMEM((z.ng,) + unit, BF),
        midb=pltpu.VMEM((z.ng,) + unit, BF),
        midq=pltpu.VMEM((z.nb, z.chips) + piece, BF),
        ownm=pltpu.VMEM((z.nb,) + piece, BF),
        og_s=pltpu.VMEM((z.nb, z.chips) + piece, BF),
        ox_s=pltpu.VMEM((z.nb, z.chips) + piece, BF),
        og_r=pltpu.VMEM((z.nb,) + piece, BF),
        ox_r=pltpu.VMEM((z.nb, z.chips) + piece, BF),
        load_sem=dma((6,)), wf_sem=dma((z.ng, 2)), store_sem=dma((z.rows // 256,)),
        halo_ss=dma((2,)), halo_rs=dma((2,)),
        pair_ss=dma((z.ng,)), pair_rs=dma((z.ng,)),
        chain_ss=dma((z.ng,)), chain_rs=dma((z.ng,)),
        mid_ss=dma((z.ng,)), mid_rs=dma((z.ng,)),
        part_ss=dma((z.ng,)), part_rs=dma((z.ng,)),
        om_ss=dma((z.nb, z.chips)), om_rs=dma((z.nb,)),
        og_ss=dma((z.nb, z.chips)), og_rs=dma((z.nb,)),
        ox_ss=dma((z.nb, z.chips)), ox_rs=dma((z.nb, z.chips)),
    )


INPUTS = ("q", "k", "v", "fq", "fk", "fv", "rate", "w", "gain")


def kernel(z, names, *refs):
    r = SimpleNamespace(**dict(zip(names, refs)))
    s = lax.axis_index("seq")
    hd = lax.axis_index("head")
    chip = lax.div(s, 2)
    c = s - 2 * chip
    b = lax.div(chip, z.chips)
    p = chip - b * z.chips
    first, second = b == 0, b == 1
    head_chip, tail_chip = p == 0, p == z.chips - 1

    def both(*conditions):
        return functools.reduce(jnp.logical_and, conditions)

    def either(*conditions):
        return functools.reduce(jnp.logical_or, conditions)

    def remote(src, dst, ss, rs, device):
        return pltpu.make_async_remote_copy(
            src_ref=src, dst_ref=dst, send_sem=ss, recv_sem=rs,
            device_id=(device, hd), device_id_type=pl.DeviceIdType.MESH,
        )

    def pair(g):
        return remote(r.pair_s.at[g], r.pair_r.at[g], r.pair_ss.at[g], r.pair_rs.at[g], s + 1 - 2 * c)

    def chain(g):
        return remote(r.chain_s.at[g], r.chain_r.at[g], r.chain_ss.at[g], r.chain_rs.at[g], s + 2 - 4 * b)

    def mid_out(g):
        return remote(r.midb.at[g], r.wb.at[g, c], r.mid_ss.at[g], r.mid_rs.at[g], s + 2)

    def mid_on(g):
        return remote(r.wb.at[g, c], r.wb.at[g, c], r.mid_ss.at[g], r.mid_rs.at[g], s + 2)

    def mid_part(g, core):
        return remote(r.wb.at[g, core], r.wb.at[g, core], r.part_ss.at[g], r.part_rs.at[g], s + 1 - 2 * c)

    def own_mid(g, t):
        return remote(r.midq.at[g, t], r.ownm.at[g], r.om_ss.at[g, t], r.om_rs.at[g], 2 * t + c)

    def own_grad(g, t):
        return remote(r.og_s.at[g, t], r.og_r.at[g], r.og_ss.at[g, t], r.og_rs.at[g], 2 * t + c)

    def cross_grad(g, t, origin):
        return remote(
            r.ox_s.at[g, t], r.ox_r.at[g, origin], r.ox_ss.at[g, t], r.ox_rs.at[g, origin],
            z.half + 2 * t + c,
        )

    def halo(n):
        src, dst = ((r.k, r.hk), (r.v, r.hv))[n]
        return remote(
            src.at[pl.ds(z.rows - WINDOW, WINDOW)], dst, r.halo_ss.at[n], r.halo_rs.at[n], s + 1
        )

    def load(n):
        src, dst = (
            (r.q, r.qs), (r.k, r.ks), (r.v, r.vs), (r.fq, r.fqs), (r.fk, r.xs), (r.fv, r.ys)
        )[n]
        return pltpu.make_async_copy(src, dst, r.load_sem.at[n])

    def load_w(g, core):
        block = lax.div(g, z.nb)
        return pltpu.make_async_copy(
            r.w.at[:, block, :, core, g - block * z.nb], r.wf.at[g, core], r.wf_sem.at[g, core]
        )

    def peer(n):
        other, core, block = n // 2, n % 2, n // z.half
        near = b == block
        if other < z.chips:
            near = either(near, chip == z.chips)
        if other == z.chips:
            near = either(near, first)
        return both(s != n, either(both(c == core, near), s == n - 1, s == n + 1))

    barrier = pltpu.get_barrier_semaphore()
    for n in range(z.count):
        @pl.when(peer(n))
        def _():
            pl.semaphore_signal(
                barrier, inc=1, device_id=(n, hd), device_id_type=pl.DeviceIdType.MESH
            )

    @pl.when(first)
    def _():
        load(4).start()
        load(5).start()

        @pl.loop(0, z.ng)
        def _(g):
            for core in range(2):
                load_w(g, core).start()

    @pl.when(second)
    def _():
        for n in (0, 1, 2):
            load(n).start()

    @pl.when(s == 0)
    def _():
        r.hk[...] = jnp.zeros_like(r.hk)
        r.hv[...] = jnp.zeros_like(r.hv)

    pl.semaphore_wait(barrier, sum(jnp.where(peer(n), 1, 0) for n in range(z.count)))

    slow_halo = both(first, c == 1, p < z.chips - 1)

    @pl.when(s < z.count - 1)
    def _():
        halo(0).start()

        @pl.when(jnp.logical_not(slow_halo))
        def _():
            halo(1).start()

    @pl.when(first)
    def _():
        for n in (0, 1, 2, 3):
            load(n).start()

    @pl.when(second)
    def _():
        for n in (4, 5, 3):
            load(n).start()

    r.app[...] = jnp.zeros_like(r.app)

    def weights(i):
        w = r.wb[pl.ds(i * PACK, PACK)].reshape(PACK * 2, 3, UNIT, z.d)
        return w

    def grad_step(i):
        n = PACK * 2
        w = weights(i)
        w_gu = w[:, 0:2].reshape(n * 2 * UNIT, z.d)
        w_down = w[:, 2].reshape(n * UNIT, z.d)
        for t in range(z.rows // TILE):
            at = pl.ds(t * TILE, TILE)
            x, y, rate = r.xs[at, :], r.ys[at, :], r.rate[:, at]
            gu = mm(w_gu, x, NT).reshape(n, 2, UNIT, TILE)
            back = mm(w_down, y, NT) * rate
            gate = gu[:, 0].reshape(n * UNIT, TILE)
            up = gu[:, 1].reshape(n * UNIT, TILE)
            sg = sigmoid(gate)
            active = gate * sg
            hidden = (active * up * rate).astype(BF)
            up_grad = (back * active).astype(BF)
            gate_grad = (back * up * (sg * (1.0 + gate * (1.0 - sg)))).astype(BF)
            both_grad = jnp.concatenate(
                [gate_grad.reshape(n, 1, UNIT, TILE), up_grad.reshape(n, 1, UNIT, TILE)], 1
            ).reshape(n * 2 * UNIT, TILE)
            wide = mm(both_grad, x, NN).reshape(PACK, 2, 2, UNIT, z.d)
            down = mm(hidden, y, NN).reshape(PACK, 2, UNIT, z.d)
            if t == 0:
                r.acc[:, :, 0:2] = wide
                r.acc[:, :, 2] = down
            else:
                r.acc[:, :, 0:2] += wide
                r.acc[:, :, 2] += down
        for k in range(PACK):
            g = i * PACK + k
            r.gsum[g] = r.acc[k, c]
            r.pair_s[g] = r.acc[k, 1 - c].astype(BF)
            pair(g).start()

    def combine(g):
        pair(g).wait_recv()
        r.gsum[g] += r.pair_r[g].astype(F32)

    def add_chain(g):
        chain(g).wait_recv()
        r.gsum[g] += r.chain_r[g].astype(F32)

    def send_chain(g):
        r.chain_s[g] = r.gsum[g].astype(BF)
        chain(g).start()

    def split(unit):
        return unit.reshape(3, z.chips, z.rpo, z.d)

    def reduce_first(i):
        for k in range(PACK):
            g = i * PACK + k
            combine(g)

            @pl.when(p > 0)
            def _():
                add_chain(g)

            send_chain(g)

    def make_middle(i):
        for k in range(PACK):
            g = i * PACK + k
            combine(g)
            add_chain(g)
            middle = renormalize(r.wf[g, c].reshape(3, UNIT, z.d), r.gsum[g])
            r.midb[g] = middle.astype(BF)
            mid_out(g).start()

            @pl.when(g < z.nb)
            def _():
                pieces = split(middle)
                for t in range(z.chips):
                    r.midq[g, t] = pieces[:, t].astype(BF)
                    if t < z.chips - 1:
                        own_mid(g, t).start()

    def relay(i):
        for k in range(PACK):
            g = i * PACK + k
            mid_on(g).wait_recv()

            @pl.when(p < z.chips - 1)
            def _():
                mid_on(g).start()

            mid_part(g, c).start()
        for k in range(PACK):
            mid_part(i * PACK + k, 1 - c).wait_recv()

    def reduce_second(i):
        for k in range(PACK):
            g = i * PACK + k
            combine(g)

            @pl.when(both(g < z.nb, tail_chip))
            def _():
                send_chain(g)

            @pl.when(g >= z.nb)
            def _():
                pieces = split(r.gsum[g])
                for t in range(z.chips):
                    @pl.when(p != t)
                    def _():
                        r.ox_s[g - z.nb, t] = pieces[:, t].astype(BF)
                        cross_grad(g - z.nb, t, p).start()

    def hand_back(i):
        for k in range(PACK):
            g = i * PACK + k

            @pl.when(g < z.nb)
            def _():
                add_chain(g)

                @pl.when(p > 0)
                def _():
                    send_chain(g)

                @pl.when(head_chip)
                def _():
                    pieces = split(r.gsum[g])
                    for t in range(z.chips):
                        r.og_s[g, t] = pieces[:, t].astype(BF)
                        own_grad(g, t).start()

    tile = WINDOW // 2

    def attention_tile(h, t, bias):
        columns = pl.ds(pl.multiple_of(h * AH, AH), AH)

        def block(ref, halo_ref, at):
            if at < 0:
                return halo_ref[(at + 2) * tile : (at + 3) * tile, columns]
            return ref[at * tile : (at + 1) * tile, columns]

        keys = [block(r.ks, r.hk, t - 2 + n) for n in range(3)]
        values = [block(r.vs, r.hv, t - 2 + n) for n in range(3)]
        biases = [bias if t - 2 + n < 0 else None for n in range(2)]
        r.att[t * tile : (t + 1) * tile, columns] = attend(
            r.qs[t * tile : (t + 1) * tile, columns], keys, values, biases
        )

    def apply_step(i):
        n = PACK * 2
        w = weights(i)
        w_gate, w_up, w_down = (w[:, m].reshape(n * UNIT, z.d) for m in range(3))
        w_gu = jnp.concatenate([w_gate, w_up], 0)
        for t in range(z.rows // TILE):
            at = pl.ds(t * TILE, TILE)
            gu = mm(r.fqs[at, :], w_gu, NT)
            gate, up = gu[:, : n * UNIT], gu[:, n * UNIT :]
            hidden = (gate * sigmoid(gate) * up).astype(BF)
            r.app[at, :] += mm(hidden, w_down, NN)

    @pl.loop(0, 2 * z.ns)
    def _(j):
        early = j < z.ns
        i = lax.rem(j, z.ns)

        @pl.when(both(second, j >= z.ns))
        def _():
            relay(i)

        @pl.when(either(both(first, j == 0), both(second, j == z.ns)))
        def _():
            load(4).wait()
            load(5).wait()

        @pl.when(either(both(second, j == 0), both(first, j == z.ns)))
        def _():
            for n in (0, 1, 2):
                load(n).wait()

        @pl.when(j == z.ns)
        def _():
            load(3).wait()

        @pl.when(both(first, early))
        def _():
            for k in range(PACK):
                g = i * PACK + k
                for core in range(2):
                    load_w(g, core).wait()
                    r.wb[g, core] = r.wf[g, core].reshape(3, UNIT, z.d).astype(BF)

        differentiate = first == early

        @pl.when(differentiate)
        def _():
            grad_step(i)

        @pl.when(both(first, p < z.chips - 1, j >= 1, j <= z.ns))
        def _():
            reduce_first(j - 1)

        @pl.when(both(slow_halo, j == z.ns + 2))
        def _():
            halo(1).start()

        @pl.when(jnp.logical_not(differentiate))
        def _():
            for t in range(2, z.rows // tile):
                attention_tile(i, t, None)

        @pl.when(j >= z.ns)
        def _():
            apply_step(i)

        @pl.when(both(first, tail_chip, j >= 3, j < 3 + z.ns))
        def _():
            make_middle(j - 3)

        @pl.when(either(both(second, j == z.ns - 1), both(first, j == 2 * z.ns - 1)))
        def _():
            @pl.when(s > 0)
            def _():
                halo(0).wait_recv()
                halo(1).wait_recv()

            bias = jnp.where(s == 0, jnp.float32(NEG), jnp.float32(0.0))

            @pl.loop(0, z.heads)
            def _(h):
                for t in range(2):
                    attention_tile(h, t, bias)

        @pl.when(both(second, j >= z.ns))
        def _():
            reduce_second(i)

        @pl.when(both(second, p < z.chips - 1, j >= z.ns + 2))
        def _():
            hand_back(j - z.ns - 2)

    def store(t):
        at = pl.ds(t * 256, 256)
        return pltpu.make_async_copy(r.outs.at[at], r.mixed.at[at], r.store_sem.at[t])

    @pl.loop(0, z.rows // 256)
    def _(t):
        at = pl.ds(t * 256, 256)
        out = r.app[at, :]
        inverse = lax.rsqrt(jnp.mean(out * out, axis=-1, keepdims=True) + EPSILON)
        r.outs[at, :] = (r.att[at, :] + out * inverse * r.gain[...]).astype(BF)
        store(t).start()

    @pl.when(first)
    def _():
        @pl.loop(0, z.nb)
        def _(g):
            @pl.when(tail_chip)
            def _():
                r.ownm[g] = r.midq[g, z.chips - 1]

            @pl.when(jnp.logical_not(tail_chip))
            def _():
                own_mid(g, 0).wait_recv()

            own_grad(g, 0).wait_recv()
            r.final[:, g] = renormalize(r.ownm[g].astype(F32), r.og_r[g].astype(F32))

    @pl.when(second)
    def _():
        @pl.loop(0, z.nb)
        def _(g):
            total, middle = split(r.gsum[g + z.nb]), split(r.wb[g + z.nb, c].astype(F32))
            mine, base = total[:, 0], middle[:, 0]
            for t in range(1, z.chips):
                mine = jnp.where(p == t, total[:, t], mine)
                base = jnp.where(p == t, middle[:, t], base)
            for t in range(z.chips):
                @pl.when(p != t)
                def _():
                    cross_grad(g, t, t).wait_recv()
            for t in range(z.chips):
                mine = mine + jnp.where(p == t, 0.0, r.ox_r[g, t].astype(F32))
            r.final[:, g] = renormalize(base, mine)

    @pl.when(s < z.count - 1)
    def _():
        halo(0).wait_send()
        halo(1).wait_send()

    @pl.loop(0, z.ng)
    def _(g):
        pair(g).wait_send()

        @pl.when(either(both(first, p < z.chips - 1), both(second, p > 0, g < z.nb)))
        def _():
            chain(g).wait_send()

        @pl.when(both(first, tail_chip))
        def _():
            mid_out(g).wait_send()

        @pl.when(both(second, p < z.chips - 1))
        def _():
            mid_on(g).wait_send()

        @pl.when(second)
        def _():
            mid_part(g, c).wait_send()

    @pl.loop(0, z.nb)
    def _(g):
        for t in range(z.chips):
            if t < z.chips - 1:
                @pl.when(both(first, tail_chip))
                def _():
                    own_mid(g, t).wait_send()

            @pl.when(both(second, head_chip))
            def _():
                own_grad(g, t).wait_send()

            @pl.when(both(second, p != t))
            def _():
                cross_grad(g, t, p).wait_send()

    @pl.loop(0, z.rows // 256)
    def _(t):
        store(t).wait()


def shards(
    attn_query, attn_key, attn_value, fast_query, fast_key, fast_value, rates, fast_weights, gain
):
    rows, d = fast_key.shape
    f = fast_weights.shape[1]
    z = sizes(lax.axis_size("seq"), rows, d, f, attn_query.shape[1])
    weights = jnp.swapaxes(fast_weights[0], 0, 1).reshape(3, 2, z.chips, 2, z.nb, z.rpo, d)
    parts = scratch(z)
    anywhere = pl.BlockSpec(memory_space=pl.ANY)
    vmem = pl.BlockSpec(memory_space=pltpu.VMEM)
    mixed, final = pl.pallas_call(
        functools.partial(kernel, z, INPUTS + ("mixed", "final") + tuple(parts)),
        out_shape=(
            jax.ShapeDtypeStruct((rows, d), BF),
            jax.ShapeDtypeStruct((3, z.nb, z.rpo, d), F32),
        ),
        in_specs=[anywhere] * 6 + [vmem, anywhere, vmem],
        out_specs=(anywhere, vmem),
        scratch_shapes=list(parts.values()),
        compiler_params=pltpu.CompilerParams(
            vmem_limit_bytes=LIMIT, collective_id=0, has_side_effects=True
        ),
    )(
        attn_query, attn_key, attn_value, fast_query, fast_key, fast_value,
        rates.reshape(1, rows), weights, gain,
    )
    return (mixed, jnp.swapaxes(final.reshape(3, z.share, d), 0, 1)[None])


def solution(mesh):
    tokens = P("seq", "head")
    in_specs = (tokens,) * 7 + (P("head", None, None, None), P("head", None))
    out_specs = (tokens, P("head", "seq", None, None))
    return jax.shard_map(shards, mesh=mesh, in_specs=in_specs, out_specs=out_specs, check_vma=False)
```

time: 211 us -> 82.4 us (0.39)
  waiting for transfers between devices: 117 us -> 0 us
  Pallas kernels: 56.5 us -> 76.5 us
  other arithmetic: 13.9 us -> 0 us
  between operations: 13.8 us -> 0.65 us
  starting transfers between devices: 4.84 us -> 0 us
    reduce_scatter x2 -> x0, waiting for transfers between devices: 44.1 us -> none  [the longest x1 44.1 us: shards(): first_part = lax.psum_scatter(first, 'seq', scatter_dimension=1, tiled=True)]
    all_gather x1 -> x0, waiting for transfers between devices: 36.9 us -> none  [shards(): lax.all_gather(middle_rows.astype(jnp.bfloat16), 'seq', axis=1, tiled=True)]
    ppermute x2 -> x0, waiting for transfers between devices: 35.6 us -> none  [shards(): lax.ppermute((attn_key[-WINDOW:], attn_value[-WINDOW:]), 'seq', pairs)]
    pallas_call x4 -> x1, Pallas kernels: 56.5 us -> 76.5 us  [shards(): pl.pallas_call(functools.partial(kernel, z, INPUTS + ('mixed', 'final') +...]
    convert_element_type x2 -> x0, other arithmetic: 4.92 us -> none  [the longest x1 4.08 us: shards(): first_cast = initial.astype(jnp.bfloat16)]
    ppermute x2 -> x0, starting transfers between devices: 4.72 us -> none  [shards(): lax.ppermute((attn_key[-WINDOW:], attn_value[-WINDOW:]), 'seq', pairs)]
    select_n x1 -> x0, other arithmetic: 4.38 us -> none  [shards(): jnp.where(seq < half, first_cast, middle_cast)]
    slice x2 -> x0, local copies, waits for them, and re-layouts: 3.13 us -> none  [the longest x1 1.98 us: shards(): attn_key[-WINDOW:]]
  transfers between devices with their start and end apart: 5 -> 0, of which waited for: 4 -> 0; matrix products, arithmetic and copies ran while one was open for 4% -> 0% of each run, Pallas kernels for 14% -> 0%
where the time goes in v1:
time: 82.4 us; the launch traced here: 81.5 us
  Pallas kernels  76.5 us (93%)
  local copies, waits for them, and re-layouts  4.35 us (5%)
    pallas_call x1, Pallas kernels, shards(): pl.pallas_call(functools.partial(kernel, z, INPUTS + ('mixed', 'final') +...  76.5 us
    unnamed x4, local copies, waits for them, and re-layouts  4.35 us

profile of v1, /device:TPU:16, one launch (start us, length us, event | category | flops | bytes accessed | tf_op | source)
XLA Modules:
  0.0 81.5 jit_solution(9386332894395614165)
XLA Ops:
  0.6 76.5 %shard_map.104 = (bf16[2048,640]{1,0:T(8,128)(2,1)}, f32[3,5,16,640]{3,2,1,0:T(8,128)}) custom-call(bf16[2048,640]{1,0:T(8,128)(2,1)} %refs_0_.1, bf16[2048,640]{1,0:T(8,128)(2,1)} %refs_1_.1, bf16[2048,640]{1,0:T(8,128)(2,1)} %refs_2_.1, bf16[2048,640]{1,0:T(8,128)(2,1)} %refs_3_.1, bf16[2048,640]{1,0:T(8,128)(2,1)} %refs_4_.1, bf16[2048,640]{1,0:T(8,128)(2,1)} %refs_5_.1, ...), custom_call_target="tpu_custom_call" | custom-call | tf_op jit(solution)/shard_map/pallas_call | solution.py:591
  77.1 0.0 copy-start
  77.2 3.5 %copy.13 = bf16[2048,640]{1,0:T(8,128)(2,1)} copy(bf16[2048,640]{1,0:T(8,128)(2,1)} %get-tuple-element.8) | data formatting | bytes 5242880
  80.7 0.0 copy-done
  80.7 0.8 %copy.14 = f32[1,80,3,640]{3,1,2,0:T(8,128)} copy(f32[1,80,3,640]{3,1,2,0:T(8,128)S(1)} %bitcast.12) | data formatting | bytes 1228800
Async XLA Ops:
  77.1 3.5 %copy-start = (f32[3,5,16,640]{3,2,1,0:T(8,128)S(1)}, f32[3,5,16,640]{3,2,1,0:T(8,128)}, u32[]{:S(2)}) copy-start(f32[3,5,16,640]{3,2,1,0:T(8,128)} %get-tuple-element.5) | copy-start | bytes 1843204

commit v2 on v1

--- a/solution.py
+++ b/solution.py
@@ -1,3 +1,4 @@
+import contextlib
 import functools
 import math
 from types import SimpleNamespace
@@ -15,14 +16,20 @@
 NEG = -1e30
 NT = (((1,), (1,)), ((), ()))
 NN = (((1,), (0,)), ((), ()))
-LIMIT = 62 * 1024 * 1024
+LIMIT = 52 * 1024 * 1024
 UNIT = 32
 PACK = 2
 TILE = 1024
+SMALL = 512
+TRACE = False
 BF = jnp.bfloat16
 F32 = jnp.float32
 
 
+def scope(name):
+    return jax.named_scope(name) if TRACE else contextlib.nullcontext()
+
+
 def mm(a, b, dims):
     return lax.dot_general(a, b, dims, preferred_element_type=jnp.float32)
 
@@ -31,9 +38,8 @@
     return 0.5 * jnp.tanh(0.5 * v) + 0.5
 
 
-def attend(q, keys, values, biases):
+def attend_scores(q, keys, biases):
     rows = q.shape[0]
-    factor = math.log2(math.e) / math.sqrt(AH)
     old, mid, new = (mm(q, k, NT) for k in keys)
     if biases[0] is not None:
         old = old + biases[0]
@@ -42,16 +48,20 @@
     row = lax.broadcasted_iota(jnp.int32, (rows, rows), 0)
     col = lax.broadcasted_iota(jnp.int32, (rows, rows), 1)
     causal = col <= row
-    edge = jnp.where(causal, new, old)
-    top = jnp.maximum(jnp.max(edge, -1, keepdims=True), jnp.max(mid, -1, keepdims=True))
+    return jnp.where(causal, new, old), mid, causal
+
+
+def attend_values(edge, mid, causal, values):
+    factor = math.log2(math.e) / math.sqrt(AH)
+    top = jnp.max(jnp.maximum(edge, mid), -1, keepdims=True)
     edge = jnp.exp2((edge - top) * factor)
     mid = jnp.exp2((mid - top) * factor)
-    total = jnp.sum(edge, -1, keepdims=True) + jnp.sum(mid, -1, keepdims=True)
     p_new = jnp.where(causal, edge, 0.0).astype(BF)
     p_old = jnp.where(causal, 0.0, edge).astype(BF)
-    out = mm(p_new, values[2], NN) + mm(p_old, values[0], NN)
-    out = out + mm(mid.astype(BF), values[1], NN)
-    return out * (1.0 / total)
+    ones = jnp.ones_like(values[0])
+    values = jnp.concatenate([jnp.concatenate([v, ones], 1) for v in values], 0)
+    out = mm(jnp.concatenate([p_old, mid.astype(BF), p_new], 1), values, NN)
+    return out[:, :AH] * (1.0 / out[:, AH:])
 
 
 def renormalize(previous, grad):
@@ -85,10 +95,10 @@
     halo = pltpu.VMEM((WINDOW, z.d), BF)
     dma = pltpu.SemaphoreType.DMA
     return dict(
-        qs=tokens, ks=tokens, vs=tokens, fqs=tokens, xs=tokens, ys=tokens, outs=tokens,
+        qs=tokens, ks=tokens, vs=tokens, fqs=tokens, xs=tokens, ys=tokens, hid=tokens, outs=tokens,
         att=pltpu.VMEM((z.rows, z.d), F32),
-        app=pltpu.VMEM((z.rows, z.d), F32),
         hk=halo, hv=halo,
+        rates=pltpu.VMEM((1, z.rows), F32), gains=pltpu.VMEM((1, z.d), F32),
         wf=pltpu.VMEM((z.ng, 2, 3, z.chips, z.rpo, z.d), F32),
         wb=pltpu.VMEM((z.ng, 2) + unit, BF),
         acc=pltpu.VMEM((PACK, 2) + unit, F32),
@@ -104,7 +114,7 @@
         ox_s=pltpu.VMEM((z.nb, z.chips) + piece, BF),
         og_r=pltpu.VMEM((z.nb,) + piece, BF),
         ox_r=pltpu.VMEM((z.nb, z.chips) + piece, BF),
-        load_sem=dma((6,)), wf_sem=dma((z.ng, 2)), store_sem=dma((z.rows // 256,)),
+        load_sem=dma((8,)), store_sem=dma((z.rows // (2 * SMALL),)), wf_sem=dma((z.ng, 2)),
         halo_ss=dma((2,)), halo_rs=dma((2,)),
         pair_ss=dma((z.ng,)), pair_rs=dma((z.ng,)),
         chain_ss=dma((z.ng,)), chain_rs=dma((z.ng,)),
@@ -177,7 +187,8 @@
 
     def load(n):
         src, dst = (
-            (r.q, r.qs), (r.k, r.ks), (r.v, r.vs), (r.fq, r.fqs), (r.fk, r.xs), (r.fv, r.ys)
+            (r.q, r.qs), (r.k, r.ks), (r.v, r.vs), (r.fq, r.fqs), (r.fk, r.xs), (r.fv, r.ys),
+            (r.rate, r.rates), (r.gain, r.gains),
         )[n]
         return pltpu.make_async_copy(src, dst, r.load_sem.at[n])
 
@@ -204,49 +215,55 @@
                 barrier, inc=1, device_id=(n, hd), device_id_type=pl.DeviceIdType.MESH
             )
 
-    @pl.when(first)
-    def _():
-        load(4).start()
-        load(5).start()
-
-        @pl.loop(0, z.ng)
+    def load_weights(low, high):
+        @pl.loop(low, high)
         def _(g):
             for core in range(2):
                 load_w(g, core).start()
 
+    @pl.when(first)
+    def _():
+        load_weights(0, PACK)
+        for n in (4, 6, 5):
+            load(n).start()
+
     @pl.when(second)
     def _():
-        for n in (0, 1, 2):
+        for n in (1, 0, 2, 6):
             load(n).start()
+
+    load(7).start()
 
     @pl.when(s == 0)
     def _():
         r.hk[...] = jnp.zeros_like(r.hk)
         r.hv[...] = jnp.zeros_like(r.hv)
 
-    pl.semaphore_wait(barrier, sum(jnp.where(peer(n), 1, 0) for n in range(z.count)))
-
-    slow_halo = both(first, c == 1, p < z.chips - 1)
-
-    @pl.when(s < z.count - 1)
-    def _():
-        halo(0).start()
-
-        @pl.when(jnp.logical_not(slow_halo))
+    late_key = both(first, c == 1, p < z.chips - 1)
+    late_value = both(first, c == 1)
+
+    def enter():
+        pl.semaphore_wait(barrier, sum(jnp.where(peer(n), 1, 0) for n in range(z.count)))
+
+        @pl.when(both(s < z.count - 1, jnp.logical_not(late_key)))
+        def _():
+            halo(0).start()
+
+        @pl.when(both(s < z.count - 1, jnp.logical_not(late_value)))
         def _():
             halo(1).start()
 
-    @pl.when(first)
-    def _():
-        for n in (0, 1, 2, 3):
-            load(n).start()
-
-    @pl.when(second)
-    def _():
-        for n in (4, 5, 3):
-            load(n).start()
-
-    r.app[...] = jnp.zeros_like(r.app)
+        @pl.when(first)
+        def _():
+            for n in (0, 1, 2, 3):
+                load(n).start()
+
+        @pl.when(second)
+        def _():
+            for n in (4, 5, 3):
+                load(n).start()
+
+        load(7).wait()
 
     def weights(i):
         w = r.wb[pl.ds(i * PACK, PACK)].reshape(PACK * 2, 3, UNIT, z.d)
@@ -257,11 +274,22 @@
         w = weights(i)
         w_gu = w[:, 0:2].reshape(n * 2 * UNIT, z.d)
         w_down = w[:, 2].reshape(n * UNIT, z.d)
-        for t in range(z.rows // TILE):
-            at = pl.ds(t * TILE, TILE)
-            x, y, rate = r.xs[at, :], r.ys[at, :], r.rate[:, at]
-            gu = mm(w_gu, x, NT).reshape(n, 2, UNIT, TILE)
-            back = mm(w_down, y, NT) * rate
+        tiles = z.rows // TILE
+
+        def rows(ref, t):
+            return ref[t * TILE : (t + 1) * TILE, :]
+
+        def products(t):
+            return mm(w_gu, rows(r.xs, t), NT), mm(w_down, rows(r.ys, t), NT)
+
+        ahead = products(0)
+        for t in range(tiles):
+            gu, back = ahead
+            if t + 1 < tiles:
+                ahead = products(t + 1)
+            rate = r.rates[:, t * TILE : (t + 1) * TILE]
+            gu = gu.reshape(n, 2, UNIT, TILE)
+            back = back * rate
             gate = gu[:, 0].reshape(n * UNIT, TILE)
             up = gu[:, 1].reshape(n * UNIT, TILE)
             sg = sigmoid(gate)
@@ -272,8 +300,8 @@
             both_grad = jnp.concatenate(
                 [gate_grad.reshape(n, 1, UNIT, TILE), up_grad.reshape(n, 1, UNIT, TILE)], 1
             ).reshape(n * 2 * UNIT, TILE)
-            wide = mm(both_grad, x, NN).reshape(PACK, 2, 2, UNIT, z.d)
-            down = mm(hidden, y, NN).reshape(PACK, 2, UNIT, z.d)
+            wide = mm(both_grad, rows(r.xs, t), NN).reshape(PACK, 2, 2, UNIT, z.d)
+            down = mm(hidden, rows(r.ys, t), NN).reshape(PACK, 2, UNIT, z.d)
             if t == 0:
                 r.acc[:, :, 0:2] = wide
                 r.acc[:, :, 2] = down
@@ -284,7 +312,6 @@
             g = i * PACK + k
             r.gsum[g] = r.acc[k, c]
             r.pair_s[g] = r.acc[k, 1 - c].astype(BF)
-            pair(g).start()
 
     def combine(g):
         pair(g).wait_recv()
@@ -329,18 +356,14 @@
                     if t < z.chips - 1:
                         own_mid(g, t).start()
 
-    def relay(i):
-        for k in range(PACK):
-            g = i * PACK + k
-            mid_on(g).wait_recv()
-
-            @pl.when(p < z.chips - 1)
-            def _():
-                mid_on(g).start()
-
-            mid_part(g, c).start()
-        for k in range(PACK):
-            mid_part(i * PACK + k, 1 - c).wait_recv()
+    def relay(g):
+        mid_on(g).wait_recv()
+
+        @pl.when(p < z.chips - 1)
+        def _():
+            mid_on(g).start()
+
+        mid_part(g, c).start()
 
     def reduce_second(i):
         for k in range(PACK):
@@ -358,6 +381,9 @@
                     @pl.when(p != t)
                     def _():
                         r.ox_s[g - z.nb, t] = pieces[:, t].astype(BF)
+
+                    @pl.when(p > t)
+                    def _():
                         cross_grad(g - z.nb, t, p).start()
 
     def hand_back(i):
@@ -381,7 +407,7 @@
 
     tile = WINDOW // 2
 
-    def attention_tile(h, t, bias):
+    def attention_tiles(h, tiles, bias):
         columns = pl.ds(pl.multiple_of(h * AH, AH), AH)
 
         def block(ref, halo_ref, at):
@@ -389,38 +415,46 @@
                 return halo_ref[(at + 2) * tile : (at + 3) * tile, columns]
             return ref[at * tile : (at + 1) * tile, columns]
 
-        keys = [block(r.ks, r.hk, t - 2 + n) for n in range(3)]
-        values = [block(r.vs, r.hv, t - 2 + n) for n in range(3)]
-        biases = [bias if t - 2 + n < 0 else None for n in range(2)]
-        r.att[t * tile : (t + 1) * tile, columns] = attend(
-            r.qs[t * tile : (t + 1) * tile, columns], keys, values, biases
-        )
-
-    def apply_step(i):
-        n = PACK * 2
+        def scores(t):
+            keys = [block(r.ks, r.hk, t - 2 + n) for n in range(3)]
+            biases = [bias if t - 2 + n < 0 else None for n in range(2)]
+            return attend_scores(r.qs[t * tile : (t + 1) * tile, columns], keys, biases)
+
+        ahead = scores(tiles[0])
+        for n, t in enumerate(tiles):
+            now = ahead
+            if n + 1 < len(tiles):
+                ahead = scores(tiles[n + 1])
+            values = [block(r.vs, r.hv, t - 2 + m) for m in range(3)]
+            r.att[t * tile : (t + 1) * tile, columns] = attend_values(*now, values)
+
+    def hidden_step(i):
+        n = PACK * 2 * UNIT
         w = weights(i)
-        w_gate, w_up, w_down = (w[:, m].reshape(n * UNIT, z.d) for m in range(3))
-        w_gu = jnp.concatenate([w_gate, w_up], 0)
-        for t in range(z.rows // TILE):
-            at = pl.ds(t * TILE, TILE)
-            gu = mm(r.fqs[at, :], w_gu, NT)
-            gate, up = gu[:, : n * UNIT], gu[:, n * UNIT :]
-            hidden = (gate * sigmoid(gate) * up).astype(BF)
-            r.app[at, :] += mm(hidden, w_down, NN)
+        w_gu = jnp.concatenate([w[:, 0].reshape(n, z.d), w[:, 1].reshape(n, z.d)], 0)
+        columns = pl.ds(pl.multiple_of(i * n, n), n)
+        tiles = z.rows // SMALL
+
+        def products(t):
+            return mm(r.fqs[t * SMALL : (t + 1) * SMALL, :], w_gu, NT)
+
+        ahead = products(0)
+        for t in range(tiles):
+            now = ahead
+            if t + 1 < tiles:
+                ahead = products(t + 1)
+            gate, up = now[:, :n], now[:, n:]
+            r.hid[t * SMALL : (t + 1) * SMALL, columns] = (gate * sigmoid(gate) * up).astype(BF)
 
     @pl.loop(0, 2 * z.ns)
     def _(j):
-        early = j < z.ns
+        early, late = j < z.ns, j >= z.ns
         i = lax.rem(j, z.ns)
 
-        @pl.when(both(second, j >= z.ns))
-        def _():
-            relay(i)
-
         @pl.when(either(both(first, j == 0), both(second, j == z.ns)))
         def _():
-            load(4).wait()
-            load(5).wait()
+            for n in (4, 5, 6):
+                load(n).wait()
 
         @pl.when(either(both(second, j == 0), both(first, j == z.ns)))
         def _():
@@ -439,65 +473,131 @@
                     load_w(g, core).wait()
                     r.wb[g, core] = r.wf[g, core].reshape(3, UNIT, z.d).astype(BF)
 
+            @pl.when(j == 0)
+            def _():
+                load_weights(PACK, z.ng)
+
         differentiate = first == early
 
         @pl.when(differentiate)
         def _():
-            grad_step(i)
-
-        @pl.when(both(first, p < z.chips - 1, j >= 1, j <= z.ns))
-        def _():
-            reduce_first(j - 1)
-
-        @pl.when(both(slow_halo, j == z.ns + 2))
+            with scope("grad"):
+                grad_step(i)
+
+        @pl.when(jnp.logical_not(differentiate))
+        def _():
+            with scope("att"):
+                attention_tiles(i, range(2, z.rows // tile), None)
+
+        @pl.when(j == 0)
+        def _():
+            with scope("enter"):
+                enter()
+
+        @pl.when(differentiate)
+        def _():
+            for k in range(PACK):
+                pair(i * PACK + k).start()
+
+        @pl.when(both(first, p < z.chips - 1, early))
+        def _():
+            with scope("rfirst"):
+                reduce_first(i)
+
+        @pl.when(both(second, late, j < 2 * z.ns - 1))
+        def _():
+            with scope("relay0"):
+                relay((i + 1) * PACK)
+
+        @pl.when(both(late_key, j == z.ns + 1))
+        def _():
+            halo(0).start()
+
+        @pl.when(both(late_value, j == jnp.where(p < z.chips - 1, z.ns + 2, z.ns + 3)))
         def _():
             halo(1).start()
 
-        @pl.when(jnp.logical_not(differentiate))
-        def _():
-            for t in range(2, z.rows // tile):
-                attention_tile(i, t, None)
-
-        @pl.when(j >= z.ns)
-        def _():
-            apply_step(i)
-
-        @pl.when(both(first, tail_chip, j >= 3, j < 3 + z.ns))
-        def _():
-            make_middle(j - 3)
-
-        @pl.when(either(both(second, j == z.ns - 1), both(first, j == 2 * z.ns - 1)))
+        @pl.when(late)
+        def _():
+            with scope("hidden"):
+                hidden_step(i)
+
+        @pl.when(both(second, late, j < 2 * z.ns - 1))
+        def _():
+            for k in range(1, PACK):
+                with scope("relay1"):
+                    relay((i + 1) * PACK + k)
+
+        @pl.when(both(first, tail_chip, either(j == 2, both(j >= 4, j < 3 + z.ns))))
+        def _():
+            with scope("middle"):
+                make_middle(jnp.where(j == 2, 0, j - 3))
+
+        @pl.when(both(second, late))
+        def _():
+            with scope("rsecond"):
+                reduce_second(i)
+
+        @pl.when(both(second, j == 2 * z.ns - 1))
+        def _():
+            for t in range(1, z.chips):
+                @pl.when(p < t)
+                def _():
+                    @pl.loop(0, z.nb)
+                    def _(g):
+                        cross_grad(g, t, p).start()
+
+        @pl.when(both(second, p < z.chips - 1, j >= z.ns + 2))
+        def _():
+            with scope("handback"):
+                hand_back(j - z.ns - 2)
+
+        waits = either(first, s == z.half)
+
+        @pl.when(j == jnp.where(waits, 2 * z.ns - 1, z.ns - 1))
         def _():
             @pl.when(s > 0)
             def _():
-                halo(0).wait_recv()
-                halo(1).wait_recv()
+                with scope("halow"):
+                    halo(0).wait_recv()
+                    halo(1).wait_recv()
 
             bias = jnp.where(s == 0, jnp.float32(NEG), jnp.float32(0.0))
 
             @pl.loop(0, z.heads)
             def _(h):
-                for t in range(2):
-                    attention_tile(h, t, bias)
-
-        @pl.when(both(second, j >= z.ns))
-        def _():
-            reduce_second(i)
-
-        @pl.when(both(second, p < z.chips - 1, j >= z.ns + 2))
-        def _():
-            hand_back(j - z.ns - 2)
+                with scope("atth"):
+                    attention_tiles(h, range(2), bias)
+
+        @pl.when(both(second, j >= z.ns - 1, j < 2 * z.ns - 1))
+        def _():
+            base = (j + 1 - z.ns) * PACK
+
+            @pl.when(j == z.ns - 1)
+            def _():
+                relay(base)
+
+                for k in range(1, PACK):
+                    relay(base + k)
+
+            with scope("partw"):
+                for k in range(PACK):
+                    mid_part(base + k, 1 - c).wait_recv()
+
+    w_down = r.wb[:, :, 2].reshape(z.ng * 2 * UNIT, z.d)
 
     def store(t):
-        at = pl.ds(t * 256, 256)
+        at = pl.ds(pl.multiple_of(t * 2 * SMALL, 2 * SMALL), 2 * SMALL)
         return pltpu.make_async_copy(r.outs.at[at], r.mixed.at[at], r.store_sem.at[t])
 
-    @pl.loop(0, z.rows // 256)
+    @pl.loop(0, z.rows // (2 * SMALL))
     def _(t):
-        at = pl.ds(t * 256, 256)
-        out = r.app[at, :]
-        inverse = lax.rsqrt(jnp.mean(out * out, axis=-1, keepdims=True) + EPSILON)
-        r.outs[at, :] = (r.att[at, :] + out * inverse * r.gain[...]).astype(BF)
+        spots = [pl.ds(pl.multiple_of(t * 2 * SMALL + n * SMALL, SMALL), SMALL) for n in range(2)]
+        with scope("down"):
+            outs = [mm(r.hid[at, :], w_down, NN) for at in spots]
+            for at, out in zip(spots, outs):
+                inverse = lax.rsqrt(jnp.mean(out * out, axis=-1, keepdims=True) + EPSILON)
+                r.outs[at, :] = (r.att[at, :] + out * inverse * r.gains[...]).astype(BF)
         store(t).start()
 
     @pl.when(first)
@@ -510,9 +610,11 @@
 
             @pl.when(jnp.logical_not(tail_chip))
             def _():
-                own_mid(g, 0).wait_recv()
-
-            own_grad(g, 0).wait_recv()
+                with scope("ownmw"):
+                    own_mid(g, 0).wait_recv()
+
+            with scope("owngw"):
+                own_grad(g, 0).wait_recv()
             r.final[:, g] = renormalize(r.ownm[g].astype(F32), r.og_r[g].astype(F32))
 
     @pl.when(second)
@@ -527,7 +629,8 @@
             for t in range(z.chips):
                 @pl.when(p != t)
                 def _():
-                    cross_grad(g, t, t).wait_recv()
+                    with scope("crossw"):
+                        cross_grad(g, t, t).wait_recv()
             for t in range(z.chips):
                 mine = mine + jnp.where(p == t, 0.0, r.ox_r[g, t].astype(F32))
             r.final[:, g] = renormalize(base, mine)
@@ -539,7 +642,8 @@
 
     @pl.loop(0, z.ng)
     def _(g):
-        pair(g).wait_send()
+        with scope("sendw"):
+            pair(g).wait_send()
 
         @pl.when(either(both(first, p < z.chips - 1), both(second, p > 0, g < z.nb)))
         def _():
@@ -573,9 +677,10 @@
             def _():
                 cross_grad(g, t, p).wait_send()
 
-    @pl.loop(0, z.rows // 256)
+    @pl.loop(0, z.rows // (2 * SMALL))
     def _(t):
-        store(t).wait()
+        with scope("storew"):
+            store(t).wait()
 
 
 def shards(
@@ -594,7 +699,7 @@
             jax.ShapeDtypeStruct((rows, d), BF),
             jax.ShapeDtypeStruct((3, z.nb, z.rpo, d), F32),
         ),
-        in_specs=[anywhere] * 6 + [vmem, anywhere, vmem],
+        in_specs=[anywhere] * 9,
         out_specs=(anywhere, vmem),
         scratch_shapes=list(parts.values()),
         compiler_params=pltpu.CompilerParams(

time: 82.4 us -> 69.8 us (0.85)
  Pallas kernels: 76.5 us -> 63.2 us
  local copies, waits for them, and re-layouts: 4.35 us -> 5.65 us
    pallas_call x1, Pallas kernels: 76.5 us -> 63.2 us  [shards(): pl.pallas_call(functools.partial(kernel, z, INPUTS + ('mixed', 'final') +...]
    unnamed x4 -> x6, local copies, waits for them, and re-layouts: 4.35 us -> 5.65 us
where the time goes in v2:
time: 69.8 us; the launch traced here: 69.5 us
  Pallas kernels  63.2 us (91%)
  local copies, waits for them, and re-layouts  5.65 us (8%)
    pallas_call x1, Pallas kernels, shards(): pl.pallas_call(functools.partial(kernel, z, INPUTS + ('mixed', 'final') +...  63.2 us
    unnamed x6, local copies, waits for them, and re-layouts  5.65 us

profile of v2, /device:TPU:16, one launch (start us, length us, event | category | flops | bytes accessed | tf_op | source)
XLA Modules:
  0.0 69.5 jit_solution(2909301045963565973)
XLA Ops:
  0.6 0.0 copy-start
  0.6 0.7 copy-done
  1.3 0.0 copy-start.1
  1.3 0.7 copy-done.1
  2.0 63.2 %shard_map.104 = (bf16[2048,640]{1,0:T(8,128)(2,1)}, f32[3,5,16,640]{3,2,1,0:T(8,128)S(1)}) custom-call(bf16[2048,640]{1,0:T(8,128)(2,1)} %refs_0_.1, bf16[2048,640]{1,0:T(8,128)(2,1)} %refs_1_.1, bf16[2048,640]{1,0:T(8,128)(2,1)} %refs_2_.1, bf16[2048,640]{1,0:T(8,128)(2,1)} %refs_3_.1, bf16[2048,640]{1,0:T(8,128)(2,1)} %refs_4_.1, ...), custom_call_target="tpu_custom_call" | custom-call | tf_op jit(solution)/shard_map/pallas_call | solution.py:696
  65.3 3.5 %copy.13 = bf16[2048,640]{1,0:T(8,128)(2,1)} copy(bf16[2048,640]{1,0:T(8,128)(2,1)} %get-tuple-element.8) | data formatting | bytes 5242880
  68.7 0.8 %copy.14 = f32[1,80,3,640]{3,1,2,0:T(8,128)} copy(f32[1,80,3,640]{3,1,2,0:T(8,128)S(1)} %bitcast.11) | data formatting | bytes 1228800
Async XLA Ops:
  0.6 0.7 %copy-start = (f32[2048,1]{0,1:T(1,128)S(1)}, f32[2048,1]{0,1:T(1,128)}, u32[]{:S(2)}) copy-start(f32[2048,1]{0,1:T(1,128)} %param.15) | copy-start | bytes 24580
  1.3 0.7 copy-start.1

commit v3 on v2

--- a/solution.py
+++ b/solution.py
@@ -16,12 +16,13 @@
 NEG = -1e30
 NT = (((1,), (1,)), ((), ()))
 NN = (((1,), (0,)), ((), ()))
-LIMIT = 52 * 1024 * 1024
+LIMIT = 67043328
 UNIT = 32
 PACK = 2
 TILE = 1024
 SMALL = 512
 TRACE = False
+PIECES = 4
 BF = jnp.bfloat16
 F32 = jnp.float32
 
@@ -84,7 +85,7 @@
         ns=groups // PACK, rows=rows, d=d, heads=columns // AH,
     )
     assert z.rpo * z.chips == UNIT and z.nb * z.rpo == z.share and z.ns * PACK == z.ng
-    assert z.heads == z.ns and z.ns >= 3 + (z.nb - 1) // PACK
+    assert z.heads == z.ns and z.ng == 2 * z.ns and z.ns == 5 and z.rows == 2 * TILE
     return z
 
 
@@ -114,15 +115,15 @@
         ox_s=pltpu.VMEM((z.nb, z.chips) + piece, BF),
         og_r=pltpu.VMEM((z.nb,) + piece, BF),
         ox_r=pltpu.VMEM((z.nb, z.chips) + piece, BF),
-        load_sem=dma((8,)), store_sem=dma((z.rows // (2 * SMALL),)), wf_sem=dma((z.ng, 2)),
-        halo_ss=dma((2,)), halo_rs=dma((2,)),
-        pair_ss=dma((z.ng,)), pair_rs=dma((z.ng,)),
-        chain_ss=dma((z.ng,)), chain_rs=dma((z.ng,)),
-        mid_ss=dma((z.ng,)), mid_rs=dma((z.ng,)),
-        part_ss=dma((z.ng,)), part_rs=dma((z.ng,)),
-        om_ss=dma((z.nb, z.chips)), om_rs=dma((z.nb,)),
-        og_ss=dma((z.nb, z.chips)), og_rs=dma((z.nb,)),
-        ox_ss=dma((z.nb, z.chips)), ox_rs=dma((z.nb, z.chips)),
+        rows_out=pltpu.VMEM((z.nb, 3, z.rpo, z.d), F32), rows_sem=dma((1,)), load_sem=dma((10,)), store_sem=dma((1,)), wf_sem=dma((z.ns,)),
+        halo_ss=dma((4,)), halo_rs=dma((4,)),
+        pair_ss=dma((1,)), pair_rs=dma((z.ng,)),
+        chain_ss=dma((1,)), chain_rs=dma((z.ng,)),
+        mid_ss=dma((1,)), mid_rs=dma((z.ng,)),
+        part_ss=dma((1,)), part_rs=dma((z.ng,)),
+        om_ss=dma((1,)), om_rs=dma((z.nb,)),
+        og_ss=dma((1,)), og_rs=dma((z.nb,)),
+        ox_ss=dma((1,)), ox_rs=dma((z.nb, z.chips)),
     )
 
 
@@ -153,49 +154,56 @@
         )
 
     def pair(g):
-        return remote(r.pair_s.at[g], r.pair_r.at[g], r.pair_ss.at[g], r.pair_rs.at[g], s + 1 - 2 * c)
+        return remote(r.pair_s.at[g], r.pair_r.at[g], r.pair_ss.at[0], r.pair_rs.at[g], s + 1 - 2 * c)
 
     def chain(g):
-        return remote(r.chain_s.at[g], r.chain_r.at[g], r.chain_ss.at[g], r.chain_rs.at[g], s + 2 - 4 * b)
+        return remote(r.chain_s.at[g], r.chain_r.at[g], r.chain_ss.at[0], r.chain_rs.at[g], s + 2 - 4 * b)
 
     def mid_out(g):
-        return remote(r.midb.at[g], r.wb.at[g, c], r.mid_ss.at[g], r.mid_rs.at[g], s + 2)
+        return remote(r.midb.at[g], r.wb.at[g, c], r.mid_ss.at[0], r.mid_rs.at[g], s + 2)
 
     def mid_on(g):
-        return remote(r.wb.at[g, c], r.wb.at[g, c], r.mid_ss.at[g], r.mid_rs.at[g], s + 2)
+        return remote(r.wb.at[g, c], r.wb.at[g, c], r.mid_ss.at[0], r.mid_rs.at[g], s + 2)
 
     def mid_part(g, core):
-        return remote(r.wb.at[g, core], r.wb.at[g, core], r.part_ss.at[g], r.part_rs.at[g], s + 1 - 2 * c)
+        return remote(r.wb.at[g, core], r.wb.at[g, core], r.part_ss.at[0], r.part_rs.at[g], s + 1 - 2 * c)
 
     def own_mid(g, t):
-        return remote(r.midq.at[g, t], r.ownm.at[g], r.om_ss.at[g, t], r.om_rs.at[g], 2 * t + c)
+        return remote(r.midq.at[g, t], r.ownm.at[g], r.om_ss.at[0], r.om_rs.at[g], 2 * t + c)
 
     def own_grad(g, t):
-        return remote(r.og_s.at[g, t], r.og_r.at[g], r.og_ss.at[g, t], r.og_rs.at[g], 2 * t + c)
+        return remote(r.og_s.at[g, t], r.og_r.at[g], r.og_ss.at[0], r.og_rs.at[g], 2 * t + c)
 
     def cross_grad(g, t, origin):
         return remote(
-            r.ox_s.at[g, t], r.ox_r.at[g, origin], r.ox_ss.at[g, t], r.ox_rs.at[g, origin],
+            r.ox_s.at[g, t], r.ox_r.at[g, origin], r.ox_ss.at[0], r.ox_rs.at[g, origin],
             z.half + 2 * t + c,
         )
 
     def halo(n):
-        src, dst = ((r.k, r.hk), (r.v, r.hv))[n]
+        src, dst = ((r.k, r.hk), (r.v, r.hv))[n // 2]
+        half = WINDOW // 2
+        start = n % 2 * half
         return remote(
-            src.at[pl.ds(z.rows - WINDOW, WINDOW)], dst, r.halo_ss.at[n], r.halo_rs.at[n], s + 1
+            src.at[pl.ds(z.rows - WINDOW + start, half)], dst.at[pl.ds(start, half)],
+            r.halo_ss.at[n], r.halo_rs.at[n], s + 1,
         )
 
     def load(n):
         src, dst = (
-            (r.q, r.qs), (r.k, r.ks), (r.v, r.vs), (r.fq, r.fqs), (r.fk, r.xs), (r.fv, r.ys),
-            (r.rate, r.rates), (r.gain, r.gains),
+            (r.q, r.qs), (r.k, r.ks), (r.v, r.vs), (r.fq, r.fqs), (r.rate, r.rates), (r.gain, r.gains),
         )[n]
-        return pltpu.make_async_copy(src, dst, r.load_sem.at[n])
+        return pltpu.make_async_copy(src, dst, r.load_sem.at[n + n // 4 * 2])
+
+    def load_rows(n, half):
+        src, dst = ((r.fk, r.xs), (r.fv, r.ys))[n]
+        at = pl.ds(half * TILE, TILE)
+        return pltpu.make_async_copy(src.at[at], dst.at[at], r.load_sem.at[4 + n + 4 * half])
 
     def load_w(g, core):
         block = lax.div(g, z.nb)
         return pltpu.make_async_copy(
-            r.w.at[:, block, :, core, g - block * z.nb], r.wf.at[g, core], r.wf_sem.at[g, core]
+            r.w.at[:, block, :, core, g - block * z.nb], r.wf.at[g, core], r.wf_sem.at[lax.div(g, PACK)]
         )
 
     def peer(n):
@@ -224,35 +232,44 @@
     @pl.when(first)
     def _():
         load_weights(0, PACK)
-        for n in (4, 6, 5):
-            load(n).start()
+        load(4).start()
+        for half in range(2):
+            for n in range(2):
+                load_rows(n, half).start()
 
     @pl.when(second)
     def _():
-        for n in (1, 0, 2, 6):
+        for n in (1, 0, 2, 4):
             load(n).start()
 
-    load(7).start()
+    load(5).start()
 
     @pl.when(s == 0)
     def _():
         r.hk[...] = jnp.zeros_like(r.hk)
         r.hv[...] = jnp.zeros_like(r.hv)
 
-    late_key = both(first, c == 1, p < z.chips - 1)
-    late_value = both(first, c == 1)
+    sends = s < z.count - 1
+    border = both(first, c == 1, tail_chip)
+    slow = both(first, c == 1, p < z.chips - 1)
+    beside = both(first, c == 0)
+
+    def start_halo(condition, parts):
+        @pl.when(both(sends, condition))
+        def _():
+            for n in parts:
+                halo(n).start()
 
     def enter():
         pl.semaphore_wait(barrier, sum(jnp.where(peer(n), 1, 0) for n in range(z.count)))
 
-        @pl.when(both(s < z.count - 1, jnp.logical_not(late_key)))
-        def _():
-            halo(0).start()
-
-        @pl.when(both(s < z.count - 1, jnp.logical_not(late_value)))
-        def _():
-            halo(1).start()
-
+        start_halo(second, range(4))
+        start_halo(border, (0, 1))
+        start_halo(slow, (1,))
+
+        load(5).wait()
+
+    def load_rest():
         @pl.when(first)
         def _():
             for n in (0, 1, 2, 3):
@@ -260,16 +277,16 @@
 
         @pl.when(second)
         def _():
-            for n in (4, 5, 3):
-                load(n).start()
-
-        load(7).wait()
+            for half in range(2):
+                for n in range(2):
+                    load_rows(n, half).start()
+            load(3).start()
 
     def weights(i):
         w = r.wb[pl.ds(i * PACK, PACK)].reshape(PACK * 2, 3, UNIT, z.d)
         return w
 
-    def grad_step(i):
+    def grad_step(i, between):
         n = PACK * 2
         w = weights(i)
         w_gu = w[:, 0:2].reshape(n * 2 * UNIT, z.d)
@@ -282,11 +299,10 @@
         def products(t):
             return mm(w_gu, rows(r.xs, t), NT), mm(w_down, rows(r.ys, t), NT)
 
-        ahead = products(0)
         for t in range(tiles):
-            gu, back = ahead
-            if t + 1 < tiles:
-                ahead = products(t + 1)
+            if t == 1:
+                between()
+            gu, back = products(t)
             rate = r.rates[:, t * TILE : (t + 1) * TILE]
             gu = gu.reshape(n, 2, UNIT, TILE)
             back = back * rate
@@ -339,22 +355,20 @@
 
             send_chain(g)
 
-    def make_middle(i):
-        for k in range(PACK):
-            g = i * PACK + k
-            combine(g)
-            add_chain(g)
-            middle = renormalize(r.wf[g, c].reshape(3, UNIT, z.d), r.gsum[g])
-            r.midb[g] = middle.astype(BF)
-            mid_out(g).start()
-
-            @pl.when(g < z.nb)
-            def _():
-                pieces = split(middle)
-                for t in range(z.chips):
-                    r.midq[g, t] = pieces[:, t].astype(BF)
-                    if t < z.chips - 1:
-                        own_mid(g, t).start()
+    def make_middle(g):
+        combine(g)
+        add_chain(g)
+        middle = renormalize(r.wf[g, c].reshape(3, UNIT, z.d), r.gsum[g])
+        r.midb[g] = middle.astype(BF)
+        mid_out(g).start()
+
+        @pl.when(g < z.nb)
+        def _():
+            pieces = split(middle)
+            for t in range(z.chips):
+                r.midq[g, t] = pieces[:, t].astype(BF)
+                if t < z.chips - 1:
+                    own_mid(g, t).start()
 
     def relay(g):
         mid_on(g).wait_recv()
@@ -446,6 +460,22 @@
             gate, up = now[:, :n], now[:, n:]
             r.hid[t * SMALL : (t + 1) * SMALL, columns] = (gate * sigmoid(gate) * up).astype(BF)
 
+    waits = either(first, s == z.half)
+
+    def halo_tiles():
+        @pl.when(s > 0)
+        def _():
+            with scope("halow"):
+                for n in range(4):
+                    halo(n).wait_recv()
+
+        bias = jnp.where(s == 0, jnp.float32(NEG), jnp.float32(0.0))
+
+        @pl.loop(0, z.heads)
+        def _(h):
+            with scope("atth"):
+                attention_tiles(h, range(2), bias)
+
     @pl.loop(0, 2 * z.ns)
     def _(j):
         early, late = j < z.ns, j >= z.ns
@@ -453,8 +483,9 @@
 
         @pl.when(either(both(first, j == 0), both(second, j == z.ns)))
         def _():
-            for n in (4, 5, 6):
-                load(n).wait()
+            load(4).wait()
+            for n in range(2):
+                load_rows(n, 0).wait()
 
         @pl.when(either(both(second, j == 0), both(first, j == z.ns)))
         def _():
@@ -465,35 +496,79 @@
         def _():
             load(3).wait()
 
+        @pl.when(both(second, j == 0))
+        def _():
+            with scope("enter"):
+                enter()
+
         @pl.when(both(first, early))
         def _():
+            step = r.wf.at[pl.ds(i * PACK, PACK)]
+            pltpu.make_async_copy(step, step, r.wf_sem.at[i]).wait()
             for k in range(PACK):
                 g = i * PACK + k
                 for core in range(2):
-                    load_w(g, core).wait()
                     r.wb[g, core] = r.wf[g, core].reshape(3, UNIT, z.d).astype(BF)
 
             @pl.when(j == 0)
             def _():
                 load_weights(PACK, z.ng)
 
+        @pl.when(j == 1)
+        def _():
+            load_rest()
+
         differentiate = first == early
 
+        def relay_next(k, ready):
+            @pl.when(both(second, late, j < 2 * z.ns - 1, ready))
+            def _():
+                with scope("relay%d" % k):
+                    relay((i + 1) * PACK + k)
+
+        def between():
+            @pl.when(either(both(first, j == 0), both(second, j == z.ns)))
+            def _():
+                for n in range(2):
+                    load_rows(n, 1).wait()
+
+            @pl.when(both(first, j == 0))
+            def _():
+                with scope("enter"):
+                    enter()
+
+            relay_next(0, both(i > 0, p < z.chips - 1))
+
+            @pl.when(both(second, p < z.chips - 1, j >= z.ns + 3))
+            def _():
+                with scope("handback"):
+                    hand_back(j - z.ns - 3)
+
+            @pl.when(both(first, tail_chip, either(j == z.ns - 2, j == z.ns - 1)))
+            def _():
+                with scope("middle"):
+                    make_middle(j - 1)
+
+        def send_forward(low, high):
+            @pl.when(both(second, j == 2 * z.ns - 1))
+            def _():
+                for t in range(1, z.chips):
+                    @pl.when(p < t)
+                    def _():
+                        @pl.loop(low, high)
+                        def _(g):
+                            cross_grad(g, t, p).start()
+
         @pl.when(differentiate)
         def _():
             with scope("grad"):
-                grad_step(i)
+                grad_step(i, between)
 
         @pl.when(jnp.logical_not(differentiate))
         def _():
             with scope("att"):
                 attention_tiles(i, range(2, z.rows // tile), None)
 
-        @pl.when(j == 0)
-        def _():
-            with scope("enter"):
-                enter()
-
         @pl.when(differentiate)
         def _():
             for k in range(PACK):
@@ -504,70 +579,47 @@
             with scope("rfirst"):
                 reduce_first(i)
 
-        @pl.when(both(second, late, j < 2 * z.ns - 1))
-        def _():
-            with scope("relay0"):
-                relay((i + 1) * PACK)
-
-        @pl.when(both(late_key, j == z.ns + 1))
-        def _():
-            halo(0).start()
-
-        @pl.when(both(late_value, j == jnp.where(p < z.chips - 1, z.ns + 2, z.ns + 3)))
-        def _():
-            halo(1).start()
+        relay_next(0, either(i == 0, tail_chip))
+        relay_next(1, both(i == z.ns - 2, p < z.chips - 1))
+
+        start_halo(both(beside, j == z.ns + 1), range(4))
+        start_halo(both(slow, j == z.ns + 2), (0, 2, 3))
+        send_forward(0, z.nb - PACK)
+
+        @pl.when(both(first, tail_chip, j > z.ns, j < 2 * z.ns - 1))
+        def _():
+            with scope("middle"):
+                make_middle(j)
 
         @pl.when(late)
         def _():
             with scope("hidden"):
                 hidden_step(i)
 
-        @pl.when(both(second, late, j < 2 * z.ns - 1))
-        def _():
-            for k in range(1, PACK):
-                with scope("relay1"):
-                    relay((i + 1) * PACK + k)
-
-        @pl.when(both(first, tail_chip, either(j == 2, both(j >= 4, j < 3 + z.ns))))
+        relay_next(1, either(i < z.ns - 2, tail_chip))
+
+        @pl.when(both(first, tail_chip, either(j == 1, j == 2, j == z.ns - 1, j == z.ns, j == 2 * z.ns - 2)))
         def _():
             with scope("middle"):
-                make_middle(jnp.where(j == 2, 0, j - 3))
+                make_middle(jnp.where(j < 3, j - 1, jnp.where(late, j + j // (2 * z.ns - 2), j)))
 
         @pl.when(both(second, late))
         def _():
             with scope("rsecond"):
                 reduce_second(i)
 
-        @pl.when(both(second, j == 2 * z.ns - 1))
-        def _():
-            for t in range(1, z.chips):
-                @pl.when(p < t)
-                def _():
-                    @pl.loop(0, z.nb)
-                    def _(g):
-                        cross_grad(g, t, p).start()
-
-        @pl.when(both(second, p < z.chips - 1, j >= z.ns + 2))
+        send_forward(z.nb - PACK, z.nb)
+
+        @pl.when(both(second, p < z.chips - 1, j == 2 * z.ns - 1))
         def _():
             with scope("handback"):
-                hand_back(j - z.ns - 2)
-
-        waits = either(first, s == z.half)
-
-        @pl.when(j == jnp.where(waits, 2 * z.ns - 1, z.ns - 1))
-        def _():
-            @pl.when(s > 0)
-            def _():
-                with scope("halow"):
-                    halo(0).wait_recv()
-                    halo(1).wait_recv()
-
-            bias = jnp.where(s == 0, jnp.float32(NEG), jnp.float32(0.0))
-
-            @pl.loop(0, z.heads)
-            def _(h):
-                with scope("atth"):
-                    attention_tiles(h, range(2), bias)
+                hand_back(z.ns - 3)
+
+        start_halo(both(border, j == 2 * z.ns - 1), (2, 3))
+
+        @pl.when(both(jnp.logical_not(waits), j == z.ns - 1))
+        def _():
+            halo_tiles()
 
         @pl.when(both(second, j >= z.ns - 1, j < 2 * z.ns - 1))
         def _():
@@ -575,9 +627,7 @@
 
             @pl.when(j == z.ns - 1)
             def _():
-                relay(base)
-
-                for k in range(1, PACK):
+                for k in range(PACK):
                     relay(base + k)
 
             with scope("partw"):
@@ -586,101 +636,139 @@
 
     w_down = r.wb[:, :, 2].reshape(z.ng * 2 * UNIT, z.d)
 
-    def store(t):
-        at = pl.ds(pl.multiple_of(t * 2 * SMALL, 2 * SMALL), 2 * SMALL)
-        return pltpu.make_async_copy(r.outs.at[at], r.mixed.at[at], r.store_sem.at[t])
-
-    @pl.loop(0, z.rows // (2 * SMALL))
-    def _(t):
-        spots = [pl.ds(pl.multiple_of(t * 2 * SMALL + n * SMALL, SMALL), SMALL) for n in range(2)]
+    def finish(low, high):
+        spots = [pl.ds(n, SMALL) for n in range(low, high, SMALL)]
         with scope("down"):
             outs = [mm(r.hid[at, :], w_down, NN) for at in spots]
             for at, out in zip(spots, outs):
                 inverse = lax.rsqrt(jnp.mean(out * out, axis=-1, keepdims=True) + EPSILON)
                 r.outs[at, :] = (r.att[at, :] + out * inverse * r.gains[...]).astype(BF)
-        store(t).start()
-
-    @pl.when(first)
+        at = pl.ds(low, high - low)
+        pltpu.make_async_copy(r.outs.at[at], r.mixed.at[at], r.store_sem.at[0]).start()
+
+    finish(WINDOW, z.rows)
+
+    @pl.when(waits)
     def _():
-        @pl.loop(0, z.nb)
-        def _(g):
-            @pl.when(tail_chip)
-            def _():
-                r.ownm[g] = r.midq[g, z.chips - 1]
-
-            @pl.when(jnp.logical_not(tail_chip))
-            def _():
-                with scope("ownmw"):
-                    own_mid(g, 0).wait_recv()
-
-            with scope("owngw"):
-                own_grad(g, 0).wait_recv()
-            r.final[:, g] = renormalize(r.ownm[g].astype(F32), r.og_r[g].astype(F32))
-
-    @pl.when(second)
-    def _():
-        @pl.loop(0, z.nb)
-        def _(g):
-            total, middle = split(r.gsum[g + z.nb]), split(r.wb[g + z.nb, c].astype(F32))
-            mine, base = total[:, 0], middle[:, 0]
-            for t in range(1, z.chips):
-                mine = jnp.where(p == t, total[:, t], mine)
-                base = jnp.where(p == t, middle[:, t], base)
-            for t in range(z.chips):
-                @pl.when(p != t)
+        halo_tiles()
+
+    finish(0, WINDOW)
+
+    with scope("tailfin"):
+        @pl.when(first)
+        def _():
+            @pl.loop(0, z.nb)
+            def _(g):
+                @pl.when(tail_chip)
                 def _():
-                    with scope("crossw"):
-                        cross_grad(g, t, t).wait_recv()
-            for t in range(z.chips):
-                mine = mine + jnp.where(p == t, 0.0, r.ox_r[g, t].astype(F32))
-            r.final[:, g] = renormalize(base, mine)
-
-    @pl.when(s < z.count - 1)
-    def _():
-        halo(0).wait_send()
-        halo(1).wait_send()
-
-    @pl.loop(0, z.ng)
-    def _(g):
-        with scope("sendw"):
-            pair(g).wait_send()
-
-        @pl.when(either(both(first, p < z.chips - 1), both(second, p > 0, g < z.nb)))
-        def _():
-            chain(g).wait_send()
+                    r.ownm[g] = r.midq[g, z.chips - 1]
+
+                @pl.when(jnp.logical_not(tail_chip))
+                def _():
+                    with scope("ownmw"):
+                        own_mid(g, 0).wait_recv()
+
+                with scope("owngw"):
+                    own_grad(g, 0).wait_recv()
+                with scope("fin"):
+                    r.rows_out[g] = renormalize(r.ownm[g].astype(F32), r.og_r[g].astype(F32))
+                    pltpu.make_async_copy(r.rows_out.at[g], r.final.at[:, g], r.rows_sem.at[0]).start()
+
+        @pl.when(second)
+        def _():
+            @pl.loop(0, z.nb)
+            def _(g):
+                total, middle = split(r.gsum[g + z.nb]), split(r.wb[g + z.nb, c].astype(F32))
+                mine, base = total[:, 0], middle[:, 0]
+                for t in range(1, z.chips):
+                    mine = jnp.where(p == t, total[:, t], mine)
+                    base = jnp.where(p == t, middle[:, t], base)
+                for t in range(z.chips):
+                    @pl.when(p != t)
+                    def _():
+                        with scope("crossw"):
+                            cross_grad(g, t, t).wait_recv()
+                for t in range(z.chips):
+                    mine = mine + jnp.where(p == t, 0.0, r.ox_r[g, t].astype(F32))
+                with scope("fin"):
+                    r.rows_out[g] = renormalize(base, mine)
+                    pltpu.make_async_copy(r.rows_out.at[g], r.final.at[:, g], r.rows_sem.at[0]).start()
+
+    with scope("tailsend"):
+        @pl.when(s < z.count - 1)
+        def _():
+            for n in range(4):
+                halo(n).wait_send()
+
+        def sent(ref, sem):
+            remote(ref, ref, sem.at[0], sem.at[0], s).wait_send()
+
+        sent(r.pair_s, r.pair_ss)
+
+        @pl.when(both(first, p < z.chips - 1))
+        def _():
+            sent(r.chain_s, r.chain_ss)
+
+        @pl.when(both(second, p > 0))
+        def _():
+            sent(r.chain_s.at[pl.ds(0, z.nb)], r.chain_ss)
+
+        @pl.when(either(both(first, tail_chip), both(second, p < z.chips - 1)))
+        def _():
+            sent(r.midb, r.mid_ss)
+
+        @pl.when(second)
+        def _():
+            sent(r.midb, r.part_ss)
+            sent(r.ox_s.at[:, pl.ds(0, z.chips - 1)], r.ox_ss)
 
         @pl.when(both(first, tail_chip))
         def _():
-            mid_out(g).wait_send()
-
-        @pl.when(both(second, p < z.chips - 1))
-        def _():
-            mid_on(g).wait_send()
-
-        @pl.when(second)
-        def _():
-            mid_part(g, c).wait_send()
-
-    @pl.loop(0, z.nb)
-    def _(g):
-        for t in range(z.chips):
-            if t < z.chips - 1:
-                @pl.when(both(first, tail_chip))
-                def _():
-                    own_mid(g, t).wait_send()
-
-            @pl.when(both(second, head_chip))
-            def _():
-                own_grad(g, t).wait_send()
-
-            @pl.when(both(second, p != t))
-            def _():
-                cross_grad(g, t, p).wait_send()
-
-    @pl.loop(0, z.rows // (2 * SMALL))
-    def _(t):
-        with scope("storew"):
-            store(t).wait()
+            sent(r.midq.at[:, pl.ds(0, z.chips - 1)], r.om_ss)
+
+        @pl.when(both(second, head_chip))
+        def _():
+            sent(r.og_s, r.og_ss)
+
+    with scope("tailstore"):
+        pltpu.make_async_copy(r.outs, r.mixed, r.store_sem.at[0]).wait()
+        pltpu.make_async_copy(r.rows_out, r.rows_out, r.rows_sem.at[0]).wait()
+
+
+def hand_over_kernel(m_ref, f_ref, mo_ref, fo_ref, m_buf, f_buf, m_in, m_out, f_sem):
+    step = m_buf.shape[0] // PIECES
+    pieces = [pl.ds(n * step, step) for n in range(PIECES)]
+    fetches = [pltpu.make_async_copy(m_ref.at[at], m_buf.at[at], m_in.at[n]) for n, at in enumerate(pieces)]
+    stores = [pltpu.make_async_copy(m_buf.at[at], mo_ref.at[at], m_out.at[n]) for n, at in enumerate(pieces)]
+    f_fetch = pltpu.make_async_copy(f_ref, f_buf, f_sem.at[0])
+    f_store = pltpu.make_async_copy(f_buf, fo_ref, f_sem.at[1])
+    f_fetch.start()
+    for fetch in fetches:
+        fetch.start()
+    f_fetch.wait()
+    f_store.start()
+    for fetch, store in zip(fetches, stores):
+        fetch.wait()
+        store.start()
+    f_store.wait()
+    for store in stores:
+        store.wait()
+
+
+def hand_over(mixed, final):
+    hbm = pl.BlockSpec(memory_space=pltpu.HBM)
+    dma = pltpu.SemaphoreType.DMA
+    return pl.pallas_call(
+        hand_over_kernel,
+        out_shape=tuple(jax.ShapeDtypeStruct(a.shape, a.dtype) for a in (mixed, final)),
+        in_specs=[hbm] * 2,
+        out_specs=(hbm,) * 2,
+        scratch_shapes=[
+            pltpu.VMEM(mixed.shape, mixed.dtype), pltpu.VMEM(final.shape, final.dtype),
+            dma((PIECES,)), dma((PIECES,)), dma((2,)),
+        ],
+        compiler_params=pltpu.CompilerParams(vmem_limit_bytes=LIMIT),
+    )(mixed, final)
 
 
 def shards(
@@ -692,6 +780,7 @@
     weights = jnp.swapaxes(fast_weights[0], 0, 1).reshape(3, 2, z.chips, 2, z.nb, z.rpo, d)
     parts = scratch(z)
     anywhere = pl.BlockSpec(memory_space=pl.ANY)
+    hbm = pl.BlockSpec(memory_space=pltpu.HBM)
     vmem = pl.BlockSpec(memory_space=pltpu.VMEM)
     mixed, final = pl.pallas_call(
         functools.partial(kernel, z, INPUTS + ("mixed", "final") + tuple(parts)),
@@ -699,8 +788,8 @@
             jax.ShapeDtypeStruct((rows, d), BF),
             jax.ShapeDtypeStruct((3, z.nb, z.rpo, d), F32),
         ),
-        in_specs=[anywhere] * 9,
-        out_specs=(anywhere, vmem),
+        in_specs=[hbm] * 9,
+        out_specs=(anywhere, anywhere),
         scratch_shapes=list(parts.values()),
         compiler_params=pltpu.CompilerParams(
             vmem_limit_bytes=LIMIT, collective_id=0, has_side_effects=True
@@ -709,6 +798,7 @@
         attn_query, attn_key, attn_value, fast_query, fast_key, fast_value,
         rates.reshape(1, rows), weights, gain,
     )
+    mixed, final = hand_over(mixed, final)
     return (mixed, jnp.swapaxes(final.reshape(3, z.share, d), 0, 1)[None])
 
 

time: 69.8 us -> 65.6 us (0.940); the launches traced: 69.5 us -> 64.5 us
  local copies, waits for them, and re-layouts: 5.65 us -> 0 us
  Pallas kernels: 63.2 us -> 63.9 us
    unnamed x6 -> x0, local copies, waits for them, and re-layouts: 5.65 us -> none
    pallas_call x0 -> x1, Pallas kernels: none -> 3.44 us  [hand_over(): pl.pallas_call(hand_over_kernel, out_shape=tuple((jax.ShapeDtypeStruct(a....]
    pallas_call x1, Pallas kernels: 63.2 us -> 60.5 us  [shards(): pl.pallas_call(functools.partial(kernel, z, INPUTS + ('mixed', 'final') +...]
where the time goes in v3:
time: 65.6 us; the launch traced here: 64.5 us
  Pallas kernels  63.9 us (97%)
    pallas_call x1, Pallas kernels, shards(): pl.pallas_call(functools.partial(kernel, z, INPUTS + ('mixed', 'final') +...  60.5 us
    pallas_call x1, Pallas kernels, hand_over(): pl.pallas_call(hand_over_kernel, out_shape=tuple((jax.ShapeDtypeStruct(a....  3.44 us

profile of v3, /device:TPU:16, one launch (start us, length us, event | category | flops | bytes accessed | tf_op | source)
XLA Modules:
  0.0 64.5 jit_solution(11233143680353462182)
XLA Ops:
  0.6 60.5 %shard_map.104 = (bf16[2048,640]{1,0:T(8,128)(2,1)}, f32[3,5,16,640]{3,2,1,0:T(8,128)}) custom-call(bf16[2048,640]{1,0:T(8,128)(2,1)} %refs_0_.1, bf16[2048,640]{1,0:T(8,128)(2,1)} %refs_1_.1, bf16[2048,640]{1,0:T(8,128)(2,1)} %refs_2_.1, bf16[2048,640]{1,0:T(8,128)(2,1)} %refs_3_.1, bf16[2048,640]{1,0:T(8,128)(2,1)} %refs_4_.1, bf16[2048,640]{1,0:T(8,128)(2,1)} %refs_5_.1, ...), custom_call_target="tpu_custom_call" | custom-call | tf_op jit(solution)/shard_map/pallas_call | solution.py:785
  61.1 3.4 %shard_map.105 = (bf16[2048,640]{1,0:T(8,128)(2,1)}, f32[3,5,16,640]{3,2,1,0:T(8,128)}) custom-call(bf16[2048,640]{1,0:T(8,128)(2,1)} %get-tuple-element.6.m_ref, f32[3,5,16,640]{3,2,1,0:T(8,128)} %get-tuple-element.7.f_ref), custom_call_target="tpu_custom_call" | custom-call | tf_op jit(solution)/shard_map/pallas_call | solution.py:761

commit v4 on v3

--- a/solution.py
+++ b/solution.py
@@ -537,7 +537,7 @@
                 with scope("enter"):
                     enter()
 
-            relay_next(0, both(i > 0, p < z.chips - 1))
+            relay_next(0, i > 0)
 
             @pl.when(both(second, p < z.chips - 1, j >= z.ns + 3))
             def _():
@@ -579,8 +579,8 @@
             with scope("rfirst"):
                 reduce_first(i)
 
-        relay_next(0, either(i == 0, tail_chip))
-        relay_next(1, both(i == z.ns - 2, p < z.chips - 1))
+        relay_next(0, i == 0)
+        relay_next(1, either(i == z.ns - 2, both(tail_chip, i > 0)))
 
         start_halo(both(beside, j == z.ns + 1), range(4))
         start_halo(both(slow, j == z.ns + 2), (0, 2, 3))
@@ -596,7 +596,7 @@
             with scope("hidden"):
                 hidden_step(i)
 
-        relay_next(1, either(i < z.ns - 2, tail_chip))
+        relay_next(1, both(i < z.ns - 2, either(i == 0, p < z.chips - 1)))
 
         @pl.when(both(first, tail_chip, either(j == 1, j == 2, j == z.ns - 1, j == z.ns, j == 2 * z.ns - 2)))
         def _():

time: 65.6 us -> 64.1 us (0.977)
  Pallas kernels: 63.9 us -> 62.4 us
    pallas_call x1, Pallas kernels: 60.5 us -> 59 us  [shards(): pl.pallas_call(functools.partial(kernel, z, INPUTS + ('mixed', 'final') +...]
where the time goes in v4:
time: 64.1 us; the launch traced here: 63.1 us
  Pallas kernels  62.4 us (97%)
    pallas_call x1, Pallas kernels, shards(): pl.pallas_call(functools.partial(kernel, z, INPUTS + ('mixed', 'final') +...  59 us
    pallas_call x1, Pallas kernels, hand_over(): pl.pallas_call(hand_over_kernel, out_shape=tuple((jax.ShapeDtypeStruct(a....  3.44 us

profile of v4, /device:TPU:16, one launch (start us, length us, event | category | flops | bytes accessed | tf_op | source)
XLA Modules:
  0.0 63.1 jit_solution(16557057596140815054)
XLA Ops:
  0.6 59.0 %shard_map.104 = (bf16[2048,640]{1,0:T(8,128)(2,1)}, f32[3,5,16,640]{3,2,1,0:T(8,128)}) custom-call(bf16[2048,640]{1,0:T(8,128)(2,1)} %refs_0_.1, bf16[2048,640]{1,0:T(8,128)(2,1)} %refs_1_.1, bf16[2048,640]{1,0:T(8,128)(2,1)} %refs_2_.1, bf16[2048,640]{1,0:T(8,128)(2,1)} %refs_3_.1, bf16[2048,640]{1,0:T(8,128)(2,1)} %refs_4_.1, bf16[2048,640]{1,0:T(8,128)(2,1)} %refs_5_.1, ...), custom_call_target="tpu_custom_call" | custom-call | tf_op jit(solution)/shard_map/pallas_call | solution.py:785
  59.7 3.4 %shard_map.105 = (bf16[2048,640]{1,0:T(8,128)(2,1)}, f32[3,5,16,640]{3,2,1,0:T(8,128)}) custom-call(bf16[2048,640]{1,0:T(8,128)(2,1)} %get-tuple-element.6.m_ref, f32[3,5,16,640]{3,2,1,0:T(8,128)} %get-tuple-element.7.f_ref), custom_call_target="tpu_custom_call" | custom-call | tf_op jit(solution)/shard_map/pallas_call | solution.py:761

commit v5 on v4

--- a/solution.py
+++ b/solution.py
@@ -22,7 +22,7 @@
 TILE = 1024
 SMALL = 512
 TRACE = False
-PIECES = 4
+PIECES = 2
 BF = jnp.bfloat16
 F32 = jnp.float32
 
@@ -580,10 +580,15 @@
                 reduce_first(i)
 
         relay_next(0, i == 0)
-        relay_next(1, either(i == z.ns - 2, both(tail_chip, i > 0)))
+        relay_next(1, either(i >= z.ns - 3, both(tail_chip, i > 0)))
 
         start_halo(both(beside, j == z.ns + 1), range(4))
         start_halo(both(slow, j == z.ns + 2), (0, 2, 3))
+        @pl.when(both(second, p < z.chips - 1, j == 2 * z.ns - 1))
+        def _():
+            with scope("handback"):
+                hand_back(z.ns - 3)
+
         send_forward(0, z.nb - PACK)
 
         @pl.when(both(first, tail_chip, j > z.ns, j < 2 * z.ns - 1))
@@ -596,7 +601,7 @@
             with scope("hidden"):
                 hidden_step(i)
 
-        relay_next(1, both(i < z.ns - 2, either(i == 0, p < z.chips - 1)))
+        relay_next(1, both(i < z.ns - 3, either(i == 0, p < z.chips - 1)))
 
         @pl.when(both(first, tail_chip, either(j == 1, j == 2, j == z.ns - 1, j == z.ns, j == 2 * z.ns - 2)))
         def _():
@@ -609,11 +614,6 @@
                 reduce_second(i)
 
         send_forward(z.nb - PACK, z.nb)
-
-        @pl.when(both(second, p < z.chips - 1, j == 2 * z.ns - 1))
-        def _():
-            with scope("handback"):
-                hand_back(z.ns - 3)
 
         start_halo(both(border, j == 2 * z.ns - 1), (2, 3))
 

time: 64.1 us -> 63.7 us (level)
  no operation moved by 1% of the time
where the time goes in v5:
time: 63.7 us; the launch traced here: 62.7 us
  Pallas kernels  62.1 us (97%)
  between operations  0.64 us (1%)
    pallas_call x1, Pallas kernels, shards(): pl.pallas_call(functools.partial(kernel, z, INPUTS + ('mixed', 'final') +...  58.9 us
    pallas_call x1, Pallas kernels, hand_over(): pl.pallas_call(hand_over_kernel, out_shape=tuple((jax.ShapeDtypeStruct(a....  3.21 us

profile of v5, /device:TPU:16, one launch (start us, length us, event | category | flops | bytes accessed | tf_op | source)
XLA Modules:
  0.0 62.7 jit_solution(10039210616626120320)
XLA Ops:
  0.6 58.9 %shard_map.104 = (bf16[2048,640]{1,0:T(8,128)(2,1)}, f32[3,5,16,640]{3,2,1,0:T(8,128)}) custom-call(bf16[2048,640]{1,0:T(8,128)(2,1)} %refs_0_.1, bf16[2048,640]{1,0:T(8,128)(2,1)} %refs_1_.1, bf16[2048,640]{1,0:T(8,128)(2,1)} %refs_2_.1, bf16[2048,640]{1,0:T(8,128)(2,1)} %refs_3_.1, bf16[2048,640]{1,0:T(8,128)(2,1)} %refs_4_.1, bf16[2048,640]{1,0:T(8,128)(2,1)} %refs_5_.1, ...), custom_call_target="tpu_custom_call" | custom-call | tf_op jit(solution)/shard_map/pallas_call | solution.py:785
  59.5 3.2 %shard_map.105 = (bf16[2048,640]{1,0:T(8,128)(2,1)}, f32[3,5,16,640]{3,2,1,0:T(8,128)}) custom-call(bf16[2048,640]{1,0:T(8,128)(2,1)} %get-tuple-element.6.m_ref, f32[3,5,16,640]{3,2,1,0:T(8,128)} %get-tuple-element.7.f_ref), custom_call_target="tpu_custom_call" | custom-call | tf_op jit(solution)/shard_map/pallas_call | solution.py:761
